TPU v7x, 128 devices: a whole 4x4x4 slice. The times are simulated.
128 devices in a mesh: tm: 4 (over y), sta: 32 (over x, z, core).
Axes of the slice: x: 4, y: 4, z: 4, core: 2. Of those that a mesh axis runs over, the one named last changes fastest.
Arguments:
- spectra: bfloat16 [4, 32, 2, 3, 2, 2048], P('tm', 'sta'), may hold values from -6 to 6
- pair_blocks: int32 [32, 40, 2], P('sta'), may hold values from 0 to 31, as said below
- block_count: int32 [32], P('sta'), may hold values from 1 to 40, as said below
Outputs:
- correlations: bfloat16 [32, 40, 1, 1, 3, 3, 4096], P('sta', 'tm')
Inputs may be any that keep to these rules, and one draw needn't show every extreme that they name: `pair_blocks`: among the first block_count[o] slots of all owners o, every unordered pair of two different station groups stands exactly once, in either order; later slots hold arbitrary group numbers. `block_count`: the counts sum to 496, and one owner uses all 40 slots.
All inputs are finite; a program needn't handle non-finite values.
Results may differ from a plain program's by a relative error of at most 0.014.
Values may be sent and summed in bfloat16 or wider, within the bound.
A program may use at most 64 MiB of HBM per device.

v0:
```python
import functools
import math

import jax
import jax.numpy as jnp
import numpy as np
from jax import lax
from jax.experimental import pallas as pl
from jax.experimental.pallas import tpu as pltpu
from jax.sharding import PartitionSpec as P

MESH = pl.DeviceIdType.MESH
VMEM = pltpu.VMEM
DMA = pltpu.SemaphoreType.DMA

SMOOTH = 64
epsilon = 1e-05

NY, NX, NZ, NC = 4, 4, 4, 2
CHUNKS = NY * NC
F2 = 32
LOCAL = F2 // CHUNKS
WIDTH = 2048
LAGS = 4096
STATIONS = 32
HOURS = 4
SEGS = 2
SHARE = 10
TILES = SHARE * 9 * LOCAL // 8


def constants():
    lane = np.arange(128)
    part, m, u = lane // 64, (lane // 16) % 4, lane % 16
    f1 = 4 * u + m
    fine = np.arange(128)
    angle = 2.0 * math.pi * ((f1[:, None] * fine[None, :]) % 128) / 128.0
    cos, sin = np.cos(angle), np.sin(angle)
    is_re = (part == 0)[:, None]
    first = np.concatenate([np.where(is_re, cos, -sin), np.where(is_re, sin, cos)], axis=1)
    f2 = np.arange(F2)
    turn = 2.0 * math.pi * (f2[:, None] * fine[None, :]) / LAGS
    sign = np.where(f2 % 2 == 0, 1.0, -1.0)[:, None] * WIDTH ** (-0.5)
    twiddle = np.stack([np.cos(turn) * sign, np.sin(turn) * sign], axis=0)
    twiddle = twiddle.reshape(2, CHUNKS, 1, LOCAL, 128)
    twiddle = np.broadcast_to(twiddle, (2, CHUNKS, 8 // LOCAL, LOCAL, 128))
    twiddle = twiddle.reshape(2, CHUNKS, 8, 128).transpose(1, 0, 2, 3)
    coarse = np.arange(32)
    spin = 2.0 * math.pi * ((coarse[:, None] * f2[None, :]) % 32) / 32.0
    parts = []
    for table in (np.cos(spin), -np.sin(spin)):
        block = np.zeros((2, 32, 4, CHUNKS, 2, 3, LOCAL))
        for which in range(2):
            for comp in range(3):
                block[which, :, comp, :, which, comp, :] = table.reshape(32, CHUNKS, LOCAL)
        parts.append(block.reshape(256, CHUNKS * 6 * LOCAL))
    second = np.stack(parts, axis=0)
    return (
        first.astype(jnp.bfloat16),
        twiddle.astype(np.float32),
        second.astype(jnp.bfloat16),
    )


def band():
    row = lax.broadcasted_iota(jnp.int32, (128, 128), 0)
    col = lax.broadcasted_iota(jnp.int32, (128, 128), 1)
    gap = row - col
    one, zero = jnp.float32(1.0), jnp.float32(0.0)
    same = jnp.where(jnp.abs(gap) <= SMOOTH, one, zero)
    before = jnp.where(gap >= SMOOTH, one, zero)
    after = jnp.where(gap <= -SMOOTH, one, zero)
    return jnp.concatenate([before, same, after], axis=0).astype(jnp.bfloat16)


def whiten_blocks(x_ref):
    fill = jnp.zeros((2, WIDTH), jnp.float32)
    re = jnp.concatenate([x_ref[:, 0, :].astype(jnp.float32), fill], axis=0)
    im = jnp.concatenate([x_ref[:, 1, :].astype(jnp.float32), fill], axis=0)
    blocks = WIDTH // 128

    def rows(value):
        return jnp.concatenate([value[:, 128 * k : 128 * k + 128] for k in range(blocks)], axis=0)

    re, im = rows(re), rows(im)
    amplitude = jnp.sqrt(re * re + im * im)
    high = amplitude.astype(jnp.bfloat16)
    low = (amplitude - high.astype(jnp.float32)).astype(jnp.bfloat16)
    weights = band()
    total = None
    for value in (high, low):
        value = value.astype(jnp.float32)
        edge = jnp.zeros((8, 128), jnp.float32)
        before = jnp.concatenate([edge, value[:-8]], axis=0)
        after = jnp.concatenate([value[8:], edge], axis=0)
        wide = jnp.concatenate([before, value, after], axis=1).astype(jnp.bfloat16)
        term = jnp.dot(wide, weights, preferred_element_type=jnp.float32)
        total = term if total is None else total + term
    row = lax.broadcasted_iota(jnp.int32, (128, 128), 0)
    col = lax.broadcasted_iota(jnp.int32, (128, 128), 1)
    position = (row // 8) * 128 + col
    lower = jnp.maximum(position - SMOOTH, 0)
    upper = jnp.minimum(position + SMOOTH, WIDTH - 1)
    bins = (upper - lower + 1).astype(jnp.float32)
    smoothed = total / bins
    scale = smoothed + epsilon
    return re / scale, im / scale


def exchange_kernel(x_ref, pairs_ref, daily_ref, flat, packed, every, lists, out_buf,
                    list_sem, col_send, col_recv, row_send, row_recv, fwd_send, fwd_recv,
                    day_send, day_recv, own_sem):
    y = lax.axis_index("tm")
    sta = lax.axis_index("sta")
    core = sta % NC
    column = sta // NC
    xx, zz = column // NZ, column % NZ
    chunk = NC * y + core

    def station(x_at, z_at, core_at):
        return (x_at * NZ + z_at) * NC + core_at

    x_peers = [(xx + d) % NX for d in range(1, NX)]
    z_peers = [(zz + d) % NZ for d in range(1, NZ)]
    column_peers = [
        ((y + dy) % NY, (core + dc) % NC)
        for dy, dc in ((2, 0), (2, 1), (1, 0), (1, 1), (3, 0), (3, 1), (0, 1))
    ]

    barrier = pltpu.get_barrier_semaphore()
    for y_at, core_at in column_peers:
        pl.semaphore_signal(barrier, inc=1, device_id=(y_at, station(xx, zz, core_at)), device_id_type=MESH)
    for x_at in x_peers:
        pl.semaphore_signal(barrier, inc=1, device_id=(y, station(x_at, zz, core)), device_id_type=MESH)
    for z_at in z_peers:
        pl.semaphore_signal(barrier, inc=1, device_id=(y, station(xx, z_at, core)), device_id_type=MESH)

    own_list = pltpu.make_async_copy(pairs_ref, lists.at[core], list_sem.at[0])
    own_list.start()

    white_re, white_im = whiten_blocks(x_ref)
    flat[0] = white_re
    flat[1] = white_im
    turned = []
    for row in range(SEGS * 3):
        pieces = []
        for part in range(2):
            tile = flat[part, pl.ds(row, 16, stride=8), :]
            for m in range(4):
                pieces.append(tile if m == 0 else pltpu.roll(tile, 128 - 32 * m, 1))
        stacked = jnp.concatenate(pieces, axis=0)
        turned.append(jnp.transpose(stacked, (1, 0))[:F2])
    for k in range(CHUNKS):
        for comp in range(3):
            tile = jnp.concatenate(
                [turned[seg * 3 + comp][LOCAL * k : LOCAL * k + LOCAL] for seg in range(SEGS)], axis=0
            )
            packed[k, comp] = tile.astype(jnp.bfloat16)

    pl.semaphore_wait(barrier, len(column_peers) + len(x_peers) + len(z_peers))

    list_copy = pltpu.make_async_remote_copy(
        src_ref=pairs_ref,
        dst_ref=lists.at[core],
        send_sem=list_sem.at[1],
        recv_sem=list_sem.at[2],
        device_id=(y, station(xx, zz, 1 - core)),
        device_id_type=MESH,
    )
    list_copy.start()

    column_copies = []
    for at, (y_at, core_at) in enumerate(column_peers):
        copy = pltpu.make_async_remote_copy(
            src_ref=packed.at[NC * y_at + core_at],
            dst_ref=every.at[sta, y],
            send_sem=col_send.at[at],
            recv_sem=col_recv.at[chunk],
            device_id=(y_at, station(xx, zz, core_at)),
            device_id_type=MESH,
        )
        copy.start()
        column_copies.append(copy)
    own = pltpu.make_async_copy(packed.at[chunk], every.at[sta, y], own_sem)
    own.start()
    own.wait()
    for at, (y_at, core_at) in enumerate(column_peers):
        pltpu.make_async_remote_copy(
            src_ref=packed.at[chunk],
            dst_ref=every.at[station(xx, zz, core_at), y_at],
            send_sem=col_send.at[at],
            recv_sem=col_recv.at[NC * y_at + core_at],
            device_id=(y_at, station(xx, zz, core_at)),
            device_id_type=MESH,
        ).wait_recv()

    mine = every.at[pl.ds(station(xx, zz, 0), NC)]
    row_copies = []
    for at in range(3):
        for axis in range(2):
            peer = station(x_peers[at], zz, core) if axis == 0 else station(xx, z_peers[at], core)
            slot = xx if axis == 0 else zz
            copy = pltpu.make_async_remote_copy(
                src_ref=mine,
                dst_ref=mine,
                send_sem=row_send.at[axis, at],
                recv_sem=row_recv.at[axis, slot],
                device_id=(y, peer),
                device_id_type=MESH,
            )
            copy.start()
            row_copies.append(copy)
    forward_copies = []
    for at in range(3):
        for axis in range(2):
            x_at, z_at = (x_peers[at], zz) if axis == 0 else (xx, z_peers[at])
            block = every.at[pl.ds(station(x_at, z_at, 0), NC)]
            pltpu.make_async_remote_copy(
                src_ref=mine,
                dst_ref=block,
                send_sem=row_send.at[axis, at],
                recv_sem=row_recv.at[axis, x_at if axis == 0 else z_at],
                device_id=(y, station(x_at, z_at, core)),
                device_id_type=MESH,
            ).wait_recv()
            piece = every.at[station(x_at, z_at, axis)]
            for to in range(3):
                peer = station(xx, z_peers[to], core) if axis == 0 else station(x_peers[to], zz, core)
                copy = pltpu.make_async_remote_copy(
                    src_ref=piece,
                    dst_ref=piece,
                    send_sem=fwd_send.at[axis, at, to],
                    recv_sem=fwd_recv.at[axis, x_at, z_at] if axis == 0 else fwd_recv.at[axis, x_at, z_at],
                    device_id=(y, peer),
                    device_id_type=MESH,
                )
                copy.start()
                forward_copies.append(copy)
    for x_at in x_peers:
        for z_at in z_peers:
            for axis in range(2):
                piece = every.at[station(x_at, z_at, axis)]
                relay = station(xx, z_at, core) if axis == 0 else station(x_at, zz, core)
                slot_x, slot_z = (x_at, z_at)
                pltpu.make_async_remote_copy(
                    src_ref=piece,
                    dst_ref=piece,
                    send_sem=fwd_send.at[axis, 0, 0],
                    recv_sem=fwd_recv.at[axis, slot_x, slot_z],
                    device_id=(y, relay),
                    device_id_type=MESH,
                ).wait_recv()
    own_list.wait()
    list_copy.wait_send()
    pltpu.make_async_remote_copy(
        src_ref=pairs_ref,
        dst_ref=lists.at[1 - core],
        send_sem=list_sem.at[1],
        recv_sem=list_sem.at[2],
        device_id=(y, station(xx, zz, 1 - core)),
        device_id_type=MESH,
    ).wait_recv()

    lane = lax.broadcasted_iota(jnp.int32, (8, 128), 1)
    sub = lax.broadcasted_iota(jnp.int32, (8, 128), 0)
    is_re = lane < 64
    is_low = sub < LOCAL
    sign = jnp.where(is_re, jnp.float32(-1.0), jnp.float32(1.0))

    def slot_products(first, second):
        plain, crossed = [None] * 9, [None] * 9
        for hour in range(HOURS):
            left = [every[first, hour, comp].astype(jnp.float32) for comp in range(3)]
            right = [every[second, hour, comp].astype(jnp.float32) for comp in range(3)]
            swapped = [pltpu.roll(value, 64, 1) * sign for value in left]
            for a in range(3):
                for b in range(3):
                    at = 3 * a + b
                    one, two = left[a] * right[b], swapped[a] * right[b]
                    plain[at] = one if hour == 0 else plain[at] + one
                    crossed[at] = two if hour == 0 else crossed[at] + two
        joined = []
        for at in range(9):
            keep = jnp.where(is_re, plain[at], crossed[at])
            move = jnp.where(is_re, crossed[at], plain[at])
            joined.append(keep + pltpu.roll(move, 64, 1))
        return joined

    def fill(target, core_at, first_slot):
        def step(at, carry):
            values = []
            for half in range(2):
                slot = first_slot + 2 * at + half
                values += slot_products(lists[core_at, 0, slot], lists[core_at, 1, slot])
            for tile in range(9):
                one, two = values[2 * tile], values[2 * tile + 1]
                keep = jnp.where(is_low, one, two)
                move = jnp.where(is_low, two, one)
                target[9 * at + tile] = (keep + pltpu.roll(move, LOCAL, 0)).astype(jnp.bfloat16)
            return carry

        lax.fori_loop(0, SHARE // 2, step, 0)

    def send(at):
        y_at, core_at = column_peers[at]
        copy = pltpu.make_async_remote_copy(
            src_ref=out_buf.at[at],
            dst_ref=daily_ref.at[chunk],
            send_sem=day_send.at[at],
            recv_sem=day_recv.at[chunk],
            device_id=(y_at, station(xx, zz, core_at)),
            device_id_type=MESH,
        )
        copy.start()
        return copy

    day_copies = []
    for at, (y_at, core_at) in enumerate(column_peers):
        fill(out_buf.at[at], core_at, SHARE * y_at)
        day_copies.append(send(at))
    fill(daily_ref.at[chunk], core, SHARE * y)
    for at, (y_at, core_at) in enumerate(column_peers):
        pltpu.make_async_remote_copy(
            src_ref=out_buf.at[at],
            dst_ref=daily_ref.at[NC * y_at + core_at],
            send_sem=day_send.at[at],
            recv_sem=day_recv.at[NC * y_at + core_at],
            device_id=(y_at, station(xx, zz, core_at)),
            device_id_type=MESH,
        ).wait_recv()
    for copy in column_copies + row_copies + forward_copies + day_copies:
        copy.wait_send()


def lags_kernel(count_ref, daily_ref, first_ref, twiddle_ref, second_ref, out_ref, middle):
    first_slot = lax.axis_index("tm") * SHARE
    count = count_ref[0]

    def stage_one(k, carry):
        rows = daily_ref[k].astype(jnp.float32).reshape(TILES * 8, 128).astype(jnp.bfloat16)
        product = jnp.dot(rows, first_ref[...], preferred_element_type=jnp.float32)
        re = product[:, :128].reshape(TILES, 8, 128)
        im = product[:, 128:].reshape(TILES, 8, 128)
        turn_re, turn_im = twiddle_ref[k, 0], twiddle_ref[k, 1]
        middle[k, 0] = (re * turn_re - im * turn_im).reshape(TILES * 8, 128)
        middle[k, 1] = (re * turn_im + im * turn_re).reshape(TILES * 8, 128)
        return carry

    lax.fori_loop(0, CHUNKS, stage_one, 0)
    rows_of_group = 6 * LOCAL

    def stage_two(group, carry):
        at = pl.multiple_of(group * rows_of_group, 8)
        total = None
        for part in range(2):
            column = jnp.concatenate(
                [middle[k, part, pl.ds(at, rows_of_group), :] for k in range(CHUNKS)], axis=0
            ).astype(jnp.bfloat16)
            term = jnp.dot(second_ref[part], column, preferred_element_type=jnp.float32)
            total = term if total is None else total + term
        for which in range(2):
            index = 2 * group + which
            live = (first_slot + index // 3) < count
            for coarse in range(32):
                start = 128 * which + 4 * coarse
                value = total[start : start + 3]
                value = jnp.where(live, value, jnp.zeros_like(value))
                out_ref[index, :, 128 * coarse : 128 * coarse + 128] = value.astype(jnp.bfloat16)
        return carry

    lax.fori_loop(0, SHARE * 3 // 2, stage_two, 0)


def body(spectra, pair_blocks, block_count):
    values = spectra.reshape(SEGS * 3, 2, WIDTH)
    pairs = pair_blocks[0].T
    first, twiddle, second = (jnp.asarray(value) for value in constants())
    daily = pl.pallas_call(
        exchange_kernel,
        out_shape=jax.ShapeDtypeStruct((CHUNKS, TILES, 8, 128), jnp.bfloat16),
        in_specs=[
            pl.BlockSpec(memory_space=pltpu.VMEM),
            pl.BlockSpec(memory_space=pl.ANY),
        ],
        out_specs=pl.BlockSpec(memory_space=pltpu.VMEM),
        scratch_shapes=[
            VMEM((2, 128, 128), jnp.float32),
            VMEM((CHUNKS, 3, 8, 128), jnp.bfloat16),
            VMEM((STATIONS, HOURS, 3, 8, 128), jnp.bfloat16),
            pltpu.SMEM((NC,) + pairs.shape, jnp.int32),
            VMEM((CHUNKS - 1, TILES, 8, 128), jnp.bfloat16),
            DMA((3,)),
            DMA((CHUNKS - 1,)),
            DMA((CHUNKS,)),
            DMA((2, 3)),
            DMA((2, 4)),
            DMA((2, 3, 3)),
            DMA((2, 4, 4)),
            DMA((CHUNKS - 1,)),
            DMA((CHUNKS,)),
            DMA(()),
        ],
        compiler_params=pltpu.CompilerParams(collective_id=0, has_side_effects=True),
        name="exchange",
    )(values, pairs)
    lags = pl.pallas_call(
        lags_kernel,
        out_shape=jax.ShapeDtypeStruct((SHARE * 3, 3, LAGS), jnp.bfloat16),
        in_specs=[pl.BlockSpec(memory_space=pltpu.SMEM)] + [pl.BlockSpec(memory_space=pltpu.VMEM)] * 4,
        out_specs=pl.BlockSpec(memory_space=pltpu.VMEM),
        scratch_shapes=[VMEM((CHUNKS, 2, TILES * 8, 128), jnp.float32)],
        name="lags",
    )(block_count, daily, first, twiddle, second)
    return lags.reshape(1, SHARE, 1, 1, 3, 3, LAGS)


def solution(mesh):
    placed = (P("tm", "sta", None, None, None, None), P("sta", None, None), P("sta"))
    return jax.shard_map(
        body,
        mesh=mesh,
        in_specs=placed,
        out_specs=P("sta", "tm", None, None, None, None, None),
        check_vma=False,
    )
```

profile of v0, /device:TPU:1, one launch (start us, length us, event | category | flops | bytes accessed | tf_op | source)
XLA Modules:
  0.0 41.2 jit_solution(9838033972451326478)
XLA Ops:
  0.7 33.4 %exchange.1.daily_ref = bf16[8,45,8,128]{3,2,1,0:T(8,128)(2,1)} custom-call(bf16[6,2,2048]{2,1,0:T(2,128)(2,1)} %bitcast.7, s32[2,40]{1,0:T(2,128)} %bitcast.8), custom_call_target="tpu_custom_call" | custom-call | tf_op jit(solution)/shard_map/exchange/pallas_call | solution.py:378
  34.1 7.2 %lags.1 = bf16[30,3,4096]{2,1,0:T(4,128)(2,1)} custom-call(s32[1]{0:T(128)S(6)} %copy.8.count_ref, bf16[8,45,8,128]{3,2,1,0:T(8,128)(2,1)} %exchange.1.daily_ref, bf16[128,256]{1,0:T(8,128)(2,1)} %constant.6.clone.first_ref, f32[8,2,8,128]{3,2,1,0:T(8,128)} %constant.7.clone.twiddle_ref, bf16[2,256,192]{2,1,0:T(8,128)(2,1)} %constant.8.clone.second_ref), custom_call_target="tpu_custom_call" | custom-call | tf_op jit(solution)/shard_map/lags/pallas_call | solution.py:406
where the time goes:
time: 41.4 us; the launch traced here: 41.2 us
  Pallas kernels  40.6 us (98%)
  between operations  0.66 us (2%)
    pallas_call x1, Pallas kernels, body(): pl.pallas_call(exchange_kernel, out_shape=jax.ShapeDtypeStruct((CHUNKS, T...  33.4 us
    pallas_call x1, Pallas kernels, body(): pl.pallas_call(lags_kernel, out_shape=jax.ShapeDtypeStruct((SHARE * 3, 3,...  7.16 us

commit v1 on v0

v1 whole, which is shorter than its diff:
```python
import functools
import math

import jax
import jax.numpy as jnp
import numpy as np
from jax import lax
from jax.experimental import pallas as pl
from jax.experimental.pallas import tpu as pltpu
from jax.sharding import PartitionSpec as P

MESH = pl.DeviceIdType.MESH
VMEM = pltpu.VMEM
DMA = pltpu.SemaphoreType.DMA

SMOOTH = 64
epsilon = 1e-05

NY, NX, NZ, NC = 4, 4, 4, 2
CHUNKS = NY * NC
F2 = 32
LOCAL = F2 // CHUNKS
WIDTH = 2048
LAGS = 4096
STATIONS = 32
HOURS = 4
SEGS = 2
SHARE = 10
TILES = SHARE * 9 * LOCAL // 8


def constants():
    lane = np.arange(128)
    part, m, u = lane // 64, (lane // 16) % 4, lane % 16
    f1 = 4 * u + m
    fine = np.arange(128)
    angle = 2.0 * math.pi * ((f1[:, None] * fine[None, :]) % 128) / 128.0
    cos, sin = np.cos(angle), np.sin(angle)
    is_re = (part == 0)[:, None]
    first = np.concatenate([np.where(is_re, cos, -sin), np.where(is_re, sin, cos)], axis=1)
    f2 = np.arange(F2)
    turn = 2.0 * math.pi * (f2[:, None] * fine[None, :]) / LAGS
    sign = np.where(f2 % 2 == 0, 1.0, -1.0)[:, None] * WIDTH ** (-0.5)
    twiddle = np.stack([np.cos(turn) * sign, np.sin(turn) * sign], axis=0)
    twiddle = twiddle.reshape(2, CHUNKS, 1, LOCAL, 128)
    twiddle = np.broadcast_to(twiddle, (2, CHUNKS, 8 // LOCAL, LOCAL, 128))
    twiddle = twiddle.reshape(2, CHUNKS, 8, 128).transpose(1, 0, 2, 3)
    coarse = np.arange(32)
    spin = 2.0 * math.pi * ((coarse[:, None] * f2[None, :]) % 32) / 32.0
    parts = []
    for table in (np.cos(spin), -np.sin(spin)):
        block = np.zeros((2, 32, 4, CHUNKS, 2, 3, LOCAL))
        for which in range(2):
            for comp in range(3):
                block[which, :, comp, :, which, comp, :] = table.reshape(32, CHUNKS, LOCAL)
        parts.append(block.reshape(256, CHUNKS * 6 * LOCAL))
    second = np.concatenate(parts, axis=1)
    return (
        first.astype(jnp.bfloat16),
        twiddle.astype(np.float32),
        second.astype(jnp.bfloat16),
    )


def band():
    row = lax.broadcasted_iota(jnp.int32, (128, 128), 0)
    col = lax.broadcasted_iota(jnp.int32, (128, 128), 1)
    gap = row - col
    one, zero = jnp.float32(1.0), jnp.float32(0.0)
    same = jnp.where(jnp.abs(gap) <= SMOOTH, one, zero)
    before = jnp.where(gap >= SMOOTH, one, zero)
    after = jnp.where(gap <= -SMOOTH, one, zero)
    return jnp.concatenate([before, same, after], axis=0).astype(jnp.bfloat16)


def whiten_blocks(x_ref):
    fill = jnp.zeros((2, WIDTH), jnp.float32)
    re = jnp.concatenate([x_ref[:, 0, :].astype(jnp.float32), fill], axis=0)
    im = jnp.concatenate([x_ref[:, 1, :].astype(jnp.float32), fill], axis=0)
    blocks = WIDTH // 128

    def rows(value):
        return jnp.concatenate([value[:, 128 * k : 128 * k + 128] for k in range(blocks)], axis=0)

    re, im = rows(re), rows(im)
    amplitude = jnp.sqrt(re * re + im * im)
    high = amplitude.astype(jnp.bfloat16)
    low = (amplitude - high.astype(jnp.float32)).astype(jnp.bfloat16)
    weights = band()
    total = None
    for value in (high, low):
        value = value.astype(jnp.float32)
        edge = jnp.zeros((8, 128), jnp.float32)
        before = jnp.concatenate([edge, value[:-8]], axis=0)
        after = jnp.concatenate([value[8:], edge], axis=0)
        wide = jnp.concatenate([before, value, after], axis=1).astype(jnp.bfloat16)
        term = jnp.dot(wide, weights, preferred_element_type=jnp.float32)
        total = term if total is None else total + term
    row = lax.broadcasted_iota(jnp.int32, (128, 128), 0)
    col = lax.broadcasted_iota(jnp.int32, (128, 128), 1)
    position = (row // 8) * 128 + col
    lower = jnp.maximum(position - SMOOTH, 0)
    upper = jnp.minimum(position + SMOOTH, WIDTH - 1)
    bins = (upper - lower + 1).astype(jnp.float32)
    smoothed = total / bins
    scale = smoothed + epsilon
    return re / scale, im / scale


def station(x_at, z_at, core_at):
    return (x_at * NZ + z_at) * NC + core_at


def arrived(block, sem):
    pltpu.make_async_copy(block, block, sem).wait()


def kernel(count_ref, x_hbm, pairs_ref, first_hbm, twiddle_hbm, second_hbm, out_ref,
           x_ref, first_ref, twiddle_ref, second_ref,
           flat, packed, every, left, swapped, lists, out_buf, daily, middle, staged,
           const_sem, list_sem, one_send, one_recv, fwd_send, fwd_recv, day_send, day_recv, out_sem):
    y = lax.axis_index("tm")
    sta = lax.axis_index("sta")
    core = sta % NC
    column = sta // NC
    xx, zz = column // NZ, column % NZ
    chunk = NC * y + core
    place = xx * (1 - core) + zz * core

    x_peers = [(xx + d) % NX for d in (1, 3, 2)]
    z_peers = [(zz + d) % NZ for d in (1, 3, 2)]
    column_peers = [
        ((y + dy) % NY, (core + dc) % NC)
        for dy, dc in ((2, 0), (2, 1), (1, 0), (1, 1), (3, 0), (3, 1), (0, 1))
    ]

    barrier = pltpu.get_barrier_semaphore()
    greeted = 0
    for dy in range(NY):
        for core_at in (core, 1 - core):
            y_at = (y + dy) % NY
            peers = [(x_at, zz) for x_at in x_peers] + [(xx, z_at) for z_at in z_peers]
            if dy > 0 or core_at is not core:
                peers.append((xx, zz))
            for x_at, z_at in peers:
                pl.semaphore_signal(
                    barrier, inc=1, device_id=(y_at, station(x_at, z_at, core_at)), device_id_type=MESH
                )
                greeted += 1

    load = pltpu.make_async_copy(x_hbm, x_ref, const_sem.at[0])
    load.start()
    own_list = pltpu.make_async_copy(pairs_ref, lists.at[core], list_sem.at[0])
    own_list.start()
    tables = [
        pltpu.make_async_copy(first_hbm, first_ref, const_sem.at[1]),
        pltpu.make_async_copy(twiddle_hbm, twiddle_ref, const_sem.at[2]),
        pltpu.make_async_copy(second_hbm, second_ref, const_sem.at[3]),
    ]
    for table in tables:
        table.start()
    load.wait()

    white_re, white_im = whiten_blocks(x_ref)
    flat[0] = white_re
    flat[1] = white_im
    turned = []
    for row in range(SEGS * 3):
        pieces = []
        for part in range(2):
            tile = flat[part, pl.ds(row, 16, stride=8), :]
            for m in range(4):
                pieces.append(tile if m == 0 else pltpu.roll(tile, 128 - 32 * m, 1))
        stacked = jnp.concatenate(pieces, axis=0)
        turned.append(jnp.transpose(stacked, (1, 0))[:F2])
    for k in range(CHUNKS):
        for comp in range(3):
            tile = jnp.concatenate(
                [turned[seg * 3 + comp][LOCAL * k : LOCAL * k + LOCAL] for seg in range(SEGS)], axis=0
            )
            packed[k, comp] = tile.astype(jnp.bfloat16)

    pl.semaphore_wait(barrier, greeted)

    mine = every.at[xx, zz, core, y]
    one_copies = []
    for dy, di in ((2, 2), (2, 1), (2, 3), (1, 2), (3, 2), (1, 1), (3, 3), (1, 3), (3, 1),
                   (2, 0), (0, 2), (1, 0), (3, 0), (0, 1), (0, 3), (0, 0)):
        for dc in range(NC):
            if (dy, di, dc) == (0, 0, 0):
                continue
            y_at, core_at = (y + dy) % NY, (core + dc) % NC
            x_at, z_at = (xx + di * (1 - core)) % NX, (zz + di * core) % NZ
            copy = pltpu.make_async_remote_copy(
                src_ref=packed.at[NC * y_at + core_at],
                dst_ref=mine,
                send_sem=one_send.at[len(one_copies)],
                recv_sem=one_recv.at[core, place, y],
                device_id=(y_at, station(x_at, z_at, core_at)),
                device_id_type=MESH,
            )
            copy.start()
            one_copies.append(copy)
    pltpu.make_async_copy(packed.at[chunk], mine, one_recv.at[core, place, y]).start()
    list_copy = pltpu.make_async_remote_copy(
        src_ref=pairs_ref,
        dst_ref=lists.at[core],
        send_sem=list_sem.at[1],
        recv_sem=list_sem.at[2],
        device_id=(y, station(xx, zz, 1 - core)),
        device_id_type=MESH,
    )
    list_copy.start()

    lane = lax.broadcasted_iota(jnp.int32, (8, 128), 1)
    sub = lax.broadcasted_iota(jnp.int32, (8, 128), 0)
    is_re = lane < 64
    is_low = sub < LOCAL
    sign = jnp.where(is_re, jnp.float32(-1.0), jnp.float32(1.0))

    def widen(x_at, z_at, core_at):
        at = station(x_at, z_at, core_at)
        for hour in range(HOURS):
            for comp in range(3):
                value = every[x_at, z_at, core_at, hour, comp].astype(jnp.float32)
                left[at, hour, comp] = value
                swapped[at, hour, comp] = pltpu.roll(value, 64, 1) * sign

    fwd_copies = []
    here = []
    for d in (0, 1, 3, 2):
        for side in range(2):
            x_at, z_at = ((xx + d) % NX, zz) if side == 0 else (xx, (zz + d) % NZ)
            for dy in (0, 1, 3, 2):
                y_at = (y + dy) % NY
                arrived(every.at[x_at, z_at, side, y_at], one_recv.at[side, x_at if side == 0 else z_at, y_at])
            piece = every.at[x_at, z_at, side]
            for to in (2, 0, 1):
                copy = pltpu.make_async_remote_copy(
                    src_ref=piece,
                    dst_ref=piece,
                    send_sem=fwd_send.at[len(fwd_copies)],
                    recv_sem=fwd_recv.at[side, x_at, z_at],
                    device_id=(y, station(xx, z_peers[to], core) if side == 0 else station(x_peers[to], zz, core)),
                    device_id_type=MESH,
                )
                copy.start()
                fwd_copies.append(copy)
            here.append((x_at, z_at, side))
    for spot in here:
        widen(*spot)
    for to in range(3):
        for d in (0, 1, 3, 2):
            for side in range(2):
                x_at, z_at = ((xx + d) % NX, z_peers[to]) if side == 0 else (x_peers[to], (zz + d) % NZ)
                arrived(every.at[x_at, z_at, side], fwd_recv.at[side, x_at, z_at])
                widen(x_at, z_at, side)
    own_list.wait()
    arrived(lists.at[1 - core], list_sem.at[2])

    def slot_products(first, second):
        plain, crossed = [None] * 9, [None] * 9
        for hour in range(HOURS):
            one = [left[first, hour, comp] for comp in range(3)]
            turn = [swapped[first, hour, comp] for comp in range(3)]
            two = [left[second, hour, comp] for comp in range(3)]
            for a in range(3):
                for b in range(3):
                    at = 3 * a + b
                    p, q = one[a] * two[b], turn[a] * two[b]
                    plain[at] = p if hour == 0 else plain[at] + p
                    crossed[at] = q if hour == 0 else crossed[at] + q
        joined = []
        for at in range(9):
            keep = jnp.where(is_re, plain[at], crossed[at])
            move = jnp.where(is_re, crossed[at], plain[at])
            joined.append(keep + pltpu.roll(move, 64, 1))
        return joined

    def fill(target, core_at, first_slot):
        def step(at, carry):
            values = []
            for half in range(2):
                slot = first_slot + 2 * at + half
                values += slot_products(lists[core_at, 0, slot], lists[core_at, 1, slot])
            for tile in range(9):
                one, two = values[2 * tile], values[2 * tile + 1]
                keep = jnp.where(is_low, one, two)
                move = jnp.where(is_low, two, one)
                target[9 * at + tile] = (keep + pltpu.roll(move, LOCAL, 0)).astype(jnp.bfloat16)
            return carry

        lax.fori_loop(0, SHARE // 2, step, 0)

    day_copies = []
    for at, (y_at, core_at) in enumerate(column_peers):
        fill(out_buf.at[at], core_at, SHARE * y_at)
        copy = pltpu.make_async_remote_copy(
            src_ref=out_buf.at[at],
            dst_ref=daily.at[chunk],
            send_sem=day_send.at[at],
            recv_sem=day_recv.at[chunk],
            device_id=(y_at, station(xx, zz, core_at)),
            device_id_type=MESH,
        )
        copy.start()
        day_copies.append(copy)
    fill(daily.at[chunk], core, SHARE * y)

    for table in tables:
        table.wait()

    def stage_one(k):
        rows = daily[k].astype(jnp.float32).reshape(TILES * 8, 128).astype(jnp.bfloat16)
        product = jnp.dot(rows, first_ref[...], preferred_element_type=jnp.float32)
        re = product[:, :128].reshape(TILES, 8, 128)
        im = product[:, 128:].reshape(TILES, 8, 128)
        turn_re, turn_im = twiddle_ref[k, 0], twiddle_ref[k, 1]
        middle[k, 0] = (re * turn_re - im * turn_im).reshape(TILES * 8, 128)
        middle[k, 1] = (re * turn_im + im * turn_re).reshape(TILES * 8, 128)

    stage_one(chunk)
    for y_at, core_at in column_peers[::-1][:1] + column_peers[:-1]:
        k = NC * y_at + core_at
        arrived(daily.at[k], day_recv.at[k])
        stage_one(k)

    count = count_ref[0]
    first_slot = SHARE * y
    rows_of_group = 6 * LOCAL

    def group_copy(group):
        return pltpu.make_async_copy(
            staged.at[pl.ds(2 * group, 2)], out_ref.at[pl.ds(2 * group, 2)], out_sem.at[group]
        )

    def stage_two(group, carry):
        at = pl.multiple_of(group * rows_of_group, 8)
        columns = jnp.concatenate(
            [middle[k, part, pl.ds(at, rows_of_group), :] for part in range(2) for k in range(CHUNKS)], axis=0
        ).astype(jnp.bfloat16)
        total = jnp.dot(second_ref[...], columns, preferred_element_type=jnp.float32)
        for which in range(2):
            index = 2 * group + which
            live = (first_slot + index // 3) < count
            for coarse in range(32):
                start = 128 * which + 4 * coarse
                value = total[start : start + 3]
                value = jnp.where(live, value, jnp.zeros_like(value))
                staged[index, :, 128 * coarse : 128 * coarse + 128] = value.astype(jnp.bfloat16)
        group_copy(group).start()
        return carry

    groups = SHARE * 3 // 2
    lax.fori_loop(0, groups, stage_two, 0)

    def drain(group, carry):
        group_copy(group).wait()
        return carry

    lax.fori_loop(0, groups, drain, 0)
    list_copy.wait_send()
    for copy in one_copies + fwd_copies + day_copies:
        copy.wait_send()


def body(spectra, pair_blocks, block_count):
    values = spectra.reshape(SEGS * 3, 2, WIDTH)
    pairs = pair_blocks[0].T
    first, twiddle, second = (jnp.asarray(value) for value in constants())
    f32, bf16 = jnp.float32, jnp.bfloat16
    anywhere = pl.BlockSpec(memory_space=pl.ANY)
    lags = pl.pallas_call(
        kernel,
        out_shape=jax.ShapeDtypeStruct((SHARE * 3, 3, LAGS), bf16),
        in_specs=[pl.BlockSpec(memory_space=pltpu.SMEM)] + [anywhere] * 5,
        out_specs=anywhere,
        scratch_shapes=[
            VMEM(values.shape, bf16),
            VMEM(first.shape, bf16),
            VMEM(twiddle.shape, f32),
            VMEM(second.shape, bf16),
            VMEM((2, 128, 128), f32),
            VMEM((CHUNKS, 3, 8, 128), bf16),
            VMEM((NX, NZ, NC, HOURS, 3, 8, 128), bf16),
            VMEM((STATIONS, HOURS, 3, 8, 128), f32),
            VMEM((STATIONS, HOURS, 3, 8, 128), f32),
            pltpu.SMEM((NC,) + pairs.shape, jnp.int32),
            VMEM((CHUNKS - 1, TILES, 8, 128), bf16),
            VMEM((CHUNKS, TILES, 8, 128), bf16),
            VMEM((CHUNKS, 2, TILES * 8, 128), f32),
            VMEM((SHARE * 3, 3, LAGS), bf16),
            DMA((4,)),
            DMA((3,)),
            DMA((31,)),
            DMA((2, 4, 4)),
            DMA((24,)),
            DMA((2, 4, 4)),
            DMA((CHUNKS - 1,)),
            DMA((CHUNKS,)),
            DMA((SHARE * 3 // 2,)),
        ],
        compiler_params=pltpu.CompilerParams(collective_id=0, has_side_effects=True),
        name="correlate",
    )(block_count, values, pairs, first, twiddle, second)
    return lags.reshape(1, SHARE, 1, 1, 3, 3, LAGS)


def solution(mesh):
    placed = (P("tm", "sta", None, None, None, None), P("sta", None, None), P("sta"))
    return jax.shard_map(
        body,
        mesh=mesh,
        in_specs=placed,
        out_specs=P("sta", "tm", None, None, None, None, None),
        check_vma=False,
    )
```

time: 41.4 us -> 40.4 us (0.976)
  Pallas kernels: 40.6 us -> 36.9 us
  local copies, waits for them, and re-layouts: 0 us -> 2.73 us
    pallas_call x2 -> x1, Pallas kernels: 40.6 us -> 36.9 us  [body(): pl.pallas_call(kernel, out_shape=jax.ShapeDtypeStruct((SHARE * 3, 3, LAGS...]
    unnamed x0 -> x1, local copies, waits for them, and re-layouts: none -> 2.73 us
where the time goes in v1:
time: 40.4 us; the launch traced here: 40.3 us
  Pallas kernels  36.9 us (91%)
  local copies, waits for them, and re-layouts  2.73 us (7%)
  between operations  0.66 us (2%)
    pallas_call x1, Pallas kernels, body(): pl.pallas_call(kernel, out_shape=jax.ShapeDtypeStruct((SHARE * 3, 3, LAGS...  36.9 us
    unnamed x1, local copies, waits for them, and re-layouts  2.73 us

profile of v1, /device:TPU:1, one launch (start us, length us, event | category | flops | bytes accessed | tf_op | source)
XLA Modules:
  0.0 40.3 jit_solution(17939934043657074470)
XLA Ops:
  0.7 36.9 %correlate.1 = bf16[30,3,4096]{2,1,0:T(4,128)(2,1)} custom-call(s32[1]{0:T(128)S(6)} %copy.9.count_ref, bf16[6,2,2048]{2,1,0:T(2,128)(2,1)} %bitcast.8, s32[2,40]{1,0:T(2,128)} %bitcast.9, bf16[128,256]{1,0:T(8,128)(2,1)} %constant.6.clone.first_hbm, f32[8,2,8,128]{3,2,1,0:T(8,128)} %constant.7.clone.twiddle_hbm, bf16[256,384]{1,0:T(8,128)(2,1)} %constant.8.clone.second_hbm), custom_call_target="tpu_custom_call" | custom-call | tf_op jit(solution)/shard_map/correlate/pallas_call | solution.py:373
  37.6 2.7 %copy.10 = bf16[1,10,1,1,3,3,4096]{6,5,4,3,2,1,0:T(4,128)(2,1)} copy(bf16[1,10,1,1,3,3,4096]{6,5,4,3,2,1,0:T(4,128)(2,1)} %bitcast.7) | data formatting | bytes 1474560

commit v2 on v1

--- a/solution.py
+++ b/solution.py
@@ -115,9 +115,9 @@
     pltpu.make_async_copy(block, block, sem).wait()
 
 
-def kernel(count_ref, x_hbm, pairs_ref, first_hbm, twiddle_hbm, second_hbm, out_ref,
-           x_ref, first_ref, twiddle_ref, second_ref,
-           flat, packed, every, left, swapped, lists, out_buf, daily, middle, staged,
+def kernel(x_hbm, pairs_ref, first_hbm, twiddle_hbm, out_ref,
+           x_ref, first_ref, twiddle_ref, sent,
+           flat, packed, every, left, swapped, lists, out_buf, daily, middle,
            const_sem, list_sem, one_send, one_recv, fwd_send, fwd_recv, day_send, day_recv, out_sem):
     y = lax.axis_index("tm")
     sta = lax.axis_index("sta")
@@ -134,6 +134,8 @@
         for dy, dc in ((2, 0), (2, 1), (1, 0), (1, 1), (3, 0), (3, 1), (0, 1))
     ]
 
+    load = pltpu.make_async_copy(x_hbm, x_ref, const_sem.at[0])
+    load.start()
     barrier = pltpu.get_barrier_semaphore()
     greeted = 0
     for dy in range(NY):
@@ -148,14 +150,11 @@
                 )
                 greeted += 1
 
-    load = pltpu.make_async_copy(x_hbm, x_ref, const_sem.at[0])
-    load.start()
     own_list = pltpu.make_async_copy(pairs_ref, lists.at[core], list_sem.at[0])
     own_list.start()
     tables = [
         pltpu.make_async_copy(first_hbm, first_ref, const_sem.at[1]),
         pltpu.make_async_copy(twiddle_hbm, twiddle_ref, const_sem.at[2]),
-        pltpu.make_async_copy(second_hbm, second_ref, const_sem.at[3]),
     ]
     for table in tables:
         table.start()
@@ -183,7 +182,6 @@
     pl.semaphore_wait(barrier, greeted)
 
     mine = every.at[xx, zz, core, y]
-    one_copies = []
     for dy, di in ((2, 2), (2, 1), (2, 3), (1, 2), (3, 2), (1, 1), (3, 3), (1, 3), (3, 1),
                    (2, 0), (0, 2), (1, 0), (3, 0), (0, 1), (0, 3), (0, 0)):
         for dc in range(NC):
@@ -191,17 +189,15 @@
                 continue
             y_at, core_at = (y + dy) % NY, (core + dc) % NC
             x_at, z_at = (xx + di * (1 - core)) % NX, (zz + di * core) % NZ
-            copy = pltpu.make_async_remote_copy(
+            pltpu.make_async_remote_copy(
                 src_ref=packed.at[NC * y_at + core_at],
                 dst_ref=mine,
-                send_sem=one_send.at[len(one_copies)],
-                recv_sem=one_recv.at[core, place, y],
+                send_sem=one_send,
+                recv_sem=one_recv.at[core, place],
                 device_id=(y_at, station(x_at, z_at, core_at)),
                 device_id_type=MESH,
-            )
-            copy.start()
-            one_copies.append(copy)
-    pltpu.make_async_copy(packed.at[chunk], mine, one_recv.at[core, place, y]).start()
+            ).start()
+    pltpu.make_async_copy(packed.at[chunk], mine, one_recv.at[core, place]).start()
     list_copy = pltpu.make_async_remote_copy(
         src_ref=pairs_ref,
         dst_ref=lists.at[core],
@@ -226,35 +222,32 @@
                 left[at, hour, comp] = value
                 swapped[at, hour, comp] = pltpu.roll(value, 64, 1) * sign
 
-    fwd_copies = []
     here = []
     for d in (0, 1, 3, 2):
         for side in range(2):
             x_at, z_at = ((xx + d) % NX, zz) if side == 0 else (xx, (zz + d) % NZ)
-            for dy in (0, 1, 3, 2):
-                y_at = (y + dy) % NY
-                arrived(every.at[x_at, z_at, side, y_at], one_recv.at[side, x_at if side == 0 else z_at, y_at])
             piece = every.at[x_at, z_at, side]
+            arrived(piece, one_recv.at[side, x_at if side == 0 else z_at])
             for to in (2, 0, 1):
-                copy = pltpu.make_async_remote_copy(
+                pltpu.make_async_remote_copy(
                     src_ref=piece,
                     dst_ref=piece,
-                    send_sem=fwd_send.at[len(fwd_copies)],
-                    recv_sem=fwd_recv.at[side, x_at, z_at],
+                    send_sem=fwd_send,
+                    recv_sem=fwd_recv.at[side, zz if side == 0 else xx],
                     device_id=(y, station(xx, z_peers[to], core) if side == 0 else station(x_peers[to], zz, core)),
                     device_id_type=MESH,
-                )
-                copy.start()
-                fwd_copies.append(copy)
+                ).start()
             here.append((x_at, z_at, side))
     for spot in here:
         widen(*spot)
     for to in range(3):
-        for d in (0, 1, 3, 2):
-            for side in range(2):
-                x_at, z_at = ((xx + d) % NX, z_peers[to]) if side == 0 else (x_peers[to], (zz + d) % NZ)
-                arrived(every.at[x_at, z_at, side], fwd_recv.at[side, x_at, z_at])
-                widen(x_at, z_at, side)
+        for side in range(2):
+            if side == 0:
+                arrived(every.at[:, z_peers[to], 0], fwd_recv.at[0, z_peers[to]])
+            else:
+                arrived(every.at[x_peers[to], :, 1], fwd_recv.at[1, x_peers[to]])
+            for d in range(4):
+                widen(*((d, z_peers[to], 0) if side == 0 else (x_peers[to], d, 1)))
     own_list.wait()
     arrived(lists.at[1 - core], list_sem.at[2])
 
@@ -292,19 +285,16 @@
 
         lax.fori_loop(0, SHARE // 2, step, 0)
 
-    day_copies = []
     for at, (y_at, core_at) in enumerate(column_peers):
         fill(out_buf.at[at], core_at, SHARE * y_at)
-        copy = pltpu.make_async_remote_copy(
+        pltpu.make_async_remote_copy(
             src_ref=out_buf.at[at],
             dst_ref=daily.at[chunk],
-            send_sem=day_send.at[at],
+            send_sem=day_send,
             recv_sem=day_recv.at[chunk],
             device_id=(y_at, station(xx, zz, core_at)),
             device_id_type=MESH,
-        )
-        copy.start()
-        day_copies.append(copy)
+        ).start()
     fill(daily.at[chunk], core, SHARE * y)
 
     for table in tables:
@@ -316,8 +306,9 @@
         re = product[:, :128].reshape(TILES, 8, 128)
         im = product[:, 128:].reshape(TILES, 8, 128)
         turn_re, turn_im = twiddle_ref[k, 0], twiddle_ref[k, 1]
-        middle[k, 0] = (re * turn_re - im * turn_im).reshape(TILES * 8, 128)
-        middle[k, 1] = (re * turn_im + im * turn_re).reshape(TILES * 8, 128)
+        middle[k, 0] = (re * turn_re - im * turn_im).reshape(TILES * 8, 128).astype(jnp.bfloat16)
+        middle[k, 1] = (re * turn_im + im * turn_re).reshape(TILES * 8, 128).astype(jnp.bfloat16)
+        pltpu.make_async_copy(middle.at[k], out_ref.at[k], out_sem).start()
 
     stage_one(chunk)
     for y_at, core_at in column_peers[::-1][:1] + column_peers[:-1]:
@@ -325,43 +316,36 @@
         arrived(daily.at[k], day_recv.at[k])
         stage_one(k)
 
+    arrived(middle, out_sem)
+    list_copy.wait_send()
+    arrived(sent, one_send)
+    arrived(every.at[pl.ds(0, 3)], fwd_send)
+    arrived(out_buf, day_send)
+
+
+GROUPS_AT_ONCE = 5
+GROUPS = SHARE * 3 // 2
+
+
+def lags_kernel(count_ref, middle_ref, second_ref, out_ref):
+    first_slot = lax.axis_index("tm") * SHARE
     count = count_ref[0]
-    first_slot = SHARE * y
-    rows_of_group = 6 * LOCAL
-
-    def group_copy(group):
-        return pltpu.make_async_copy(
-            staged.at[pl.ds(2 * group, 2)], out_ref.at[pl.ds(2 * group, 2)], out_sem.at[group]
-        )
-
-    def stage_two(group, carry):
-        at = pl.multiple_of(group * rows_of_group, 8)
+    rows = 6 * LOCAL
+    for group in range(GROUPS_AT_ONCE):
         columns = jnp.concatenate(
-            [middle[k, part, pl.ds(at, rows_of_group), :] for part in range(2) for k in range(CHUNKS)], axis=0
+            [middle_ref[k, part, rows * group : rows * group + rows].astype(jnp.float32)
+             for part in range(2) for k in range(CHUNKS)], axis=0
         ).astype(jnp.bfloat16)
         total = jnp.dot(second_ref[...], columns, preferred_element_type=jnp.float32)
         for which in range(2):
             index = 2 * group + which
-            live = (first_slot + index // 3) < count
+            slot = first_slot + (2 * GROUPS_AT_ONCE * pl.program_id(0) + index) // 3
+            live = slot < count
             for coarse in range(32):
                 start = 128 * which + 4 * coarse
                 value = total[start : start + 3]
                 value = jnp.where(live, value, jnp.zeros_like(value))
-                staged[index, :, 128 * coarse : 128 * coarse + 128] = value.astype(jnp.bfloat16)
-        group_copy(group).start()
-        return carry
-
-    groups = SHARE * 3 // 2
-    lax.fori_loop(0, groups, stage_two, 0)
-
-    def drain(group, carry):
-        group_copy(group).wait()
-        return carry
-
-    lax.fori_loop(0, groups, drain, 0)
-    list_copy.wait_send()
-    for copy in one_copies + fwd_copies + day_copies:
-        copy.wait_send()
+                out_ref[index, :, 128 * coarse : 128 * coarse + 128] = value.astype(jnp.bfloat16)
 
 
 def body(spectra, pair_blocks, block_count):
@@ -370,16 +354,16 @@
     first, twiddle, second = (jnp.asarray(value) for value in constants())
     f32, bf16 = jnp.float32, jnp.bfloat16
     anywhere = pl.BlockSpec(memory_space=pl.ANY)
-    lags = pl.pallas_call(
+    middle = pl.pallas_call(
         kernel,
-        out_shape=jax.ShapeDtypeStruct((SHARE * 3, 3, LAGS), bf16),
-        in_specs=[pl.BlockSpec(memory_space=pltpu.SMEM)] + [anywhere] * 5,
+        out_shape=jax.ShapeDtypeStruct((CHUNKS, 2, TILES * 8, 128), bf16),
+        in_specs=[anywhere] * 4,
         out_specs=anywhere,
         scratch_shapes=[
             VMEM(values.shape, bf16),
             VMEM(first.shape, bf16),
             VMEM(twiddle.shape, f32),
-            VMEM(second.shape, bf16),
+            VMEM((31, 3, 8, 128), bf16),
             VMEM((2, 128, 128), f32),
             VMEM((CHUNKS, 3, 8, 128), bf16),
             VMEM((NX, NZ, NC, HOURS, 3, 8, 128), bf16),
@@ -388,21 +372,33 @@
             pltpu.SMEM((NC,) + pairs.shape, jnp.int32),
             VMEM((CHUNKS - 1, TILES, 8, 128), bf16),
             VMEM((CHUNKS, TILES, 8, 128), bf16),
-            VMEM((CHUNKS, 2, TILES * 8, 128), f32),
-            VMEM((SHARE * 3, 3, LAGS), bf16),
-            DMA((4,)),
+            VMEM((CHUNKS, 2, TILES * 8, 128), bf16),
             DMA((3,)),
-            DMA((31,)),
-            DMA((2, 4, 4)),
-            DMA((24,)),
-            DMA((2, 4, 4)),
-            DMA((CHUNKS - 1,)),
+            DMA((3,)),
+            DMA(()),
+            DMA((2, 4)),
+            DMA(()),
+            DMA((2, 4)),
+            DMA(()),
             DMA((CHUNKS,)),
-            DMA((SHARE * 3 // 2,)),
+            DMA(()),
         ],
         compiler_params=pltpu.CompilerParams(collective_id=0, has_side_effects=True),
         name="correlate",
-    )(block_count, values, pairs, first, twiddle, second)
+    )(values, pairs, first, twiddle)
+    at_once = GROUPS_AT_ONCE
+    lags = pl.pallas_call(
+        lags_kernel,
+        grid=(GROUPS // at_once,),
+        out_shape=jax.ShapeDtypeStruct((SHARE * 3, 3, LAGS), bf16),
+        in_specs=[
+            pl.BlockSpec(memory_space=pltpu.SMEM),
+            pl.BlockSpec((CHUNKS, 2, 6 * LOCAL * at_once, 128), lambda i: (0, 0, i, 0)),
+            pl.BlockSpec(second.shape, lambda i: (0, 0), pipeline_mode=pl.Buffered(1)),
+        ],
+        out_specs=pl.BlockSpec((2 * at_once, 3, LAGS), lambda i: (i, 0, 0)),
+        name="lags",
+    )(block_count, middle, second)
     return lags.reshape(1, SHARE, 1, 1, 3, 3, LAGS)
 
 

time: 40.4 us -> 36.9 us (0.913)
  local copies, waits for them, and re-layouts: 2.73 us -> 0 us
  Pallas kernels: 36.9 us -> 36 us
    unnamed x1 -> x0, local copies, waits for them, and re-layouts: 2.73 us -> none
    pallas_call x1 -> x2, Pallas kernels: 36.9 us -> 36 us  [the longest x1 32.2 us: body(): pl.pallas_call(kernel, out_shape=jax.ShapeDtypeStruct((CHUNKS, 2, TILES *...]
where the time goes in v2:
time: 36.9 us; the launch traced here: 36.7 us
  Pallas kernels  36 us (98%)
  between operations  0.66 us (2%)
    pallas_call x1, Pallas kernels, body(): pl.pallas_call(kernel, out_shape=jax.ShapeDtypeStruct((CHUNKS, 2, TILES *...  32.2 us
    pallas_call x1, Pallas kernels, body(): pl.pallas_call(lags_kernel, grid=(GROUPS // at_once,), out_shape=jax.Shap...  3.83 us

profile of v2, /device:TPU:1, one launch (start us, length us, event | category | flops | bytes accessed | tf_op | source)
XLA Modules:
  0.0 36.7 jit_solution(3472109917380691327)
XLA Ops:
  0.7 32.2 %correlate.1.middle_ref = bf16[8,2,360,128]{3,2,1,0:T(8,128)(2,1)} custom-call(bf16[6,2,2048]{2,1,0:T(2,128)(2,1)} %bitcast.7, s32[2,40]{1,0:T(2,128)} %bitcast.8, bf16[128,256]{1,0:T(8,128)(2,1)} %constant.6.clone.first_hbm, f32[8,2,8,128]{3,2,1,0:T(8,128)} %constant.7.clone.twiddle_hbm), custom_call_target="tpu_custom_call" | custom-call | tf_op jit(solution)/shard_map/correlate/pallas_call | solution.py:357
  32.9 3.8 %lags.1 = bf16[30,3,4096]{2,1,0:T(4,128)(2,1)} custom-call(s32[1]{0:T(128)S(6)} %copy.8.count_ref, bf16[8,2,360,128]{3,2,1,0:T(8,128)(2,1)} %correlate.1.middle_ref, bf16[256,384]{1,0:T(8,128)(2,1)} %constant.8.clone.second_ref), custom_call_target="tpu_custom_call" | custom-call | tf_op jit(solution)/shard_map/lags/pallas_call | solution.py:390

commit v3 on v2

v3 whole, which is shorter than its diff:
```python
import functools
import math

import jax
import jax.numpy as jnp
import numpy as np
from jax import lax
from jax.experimental import pallas as pl
from jax.experimental.pallas import tpu as pltpu
from jax.sharding import PartitionSpec as P

MESH = pl.DeviceIdType.MESH
VMEM = pltpu.VMEM
DMA = pltpu.SemaphoreType.DMA

SMOOTH = 64
epsilon = 1e-05

NY, NX, NZ, NC = 4, 4, 4, 2
SETS = 2
CHUNKS = 8
SOURCES = SETS * CHUNKS
F2 = 32
LOCAL = F2 // SOURCES
WIDTH = 2048
LAGS = 4096
STATIONS = 32
HOURS = 4
SEGS = 2
ROWS = SEGS * LOCAL
SHARE = 10
TILES = -(-SHARE * 9 * LOCAL // 8)
GROUPS = SHARE * 3 // 2
CUTS = (0, 5, 9, 14, 18, 23)


def constants():
    lane = np.arange(128)
    part, m, u = lane // 64, (lane // 16) % 4, lane % 16
    f1 = 4 * u + m
    fine = np.arange(128)
    angle = 2.0 * math.pi * ((f1[:, None] * fine[None, :]) % 128) / 128.0
    cos, sin = np.cos(angle), np.sin(angle)
    is_re = (part == 0)[:, None]
    first = np.concatenate([np.where(is_re, cos, -sin), np.where(is_re, sin, cos)], axis=1)
    f2 = np.arange(F2)
    turn = 2.0 * math.pi * (f2[:, None] * fine[None, :]) / LAGS
    sign = np.where(f2 % 2 == 0, 1.0, -1.0)[:, None] * WIDTH ** (-0.5)
    twiddle = np.stack([np.cos(turn) * sign, np.sin(turn) * sign], axis=0)
    twiddle = twiddle.reshape(2, SOURCES, 1, LOCAL, 128)
    twiddle = np.broadcast_to(twiddle, (2, SOURCES, 8 // LOCAL, LOCAL, 128))
    twiddle = twiddle.reshape(2, SOURCES, 8, 128).transpose(1, 0, 2, 3)
    coarse = np.arange(32)
    spin = 2.0 * math.pi * ((coarse[:, None] * f2[None, :]) % 32) / 32.0
    second = np.zeros((2, 2, 32, 4, 2, SOURCES, 8, LOCAL))
    for odd in range(2):
        for which in range(2):
            for comp in range(3):
                at = 2 * odd + 3 * which + comp
                for part_at, table in enumerate((np.cos(spin), -np.sin(spin))):
                    second[odd, which, :, comp, part_at, :, at, :] = table.reshape(32, SOURCES, LOCAL)
    second = second.reshape(2, 256, 2 * SOURCES * 8 * LOCAL)
    return (
        first.astype(jnp.bfloat16),
        twiddle.astype(np.float32),
        second.astype(jnp.bfloat16),
    )


def band():
    row = lax.broadcasted_iota(jnp.int32, (128, 128), 0)
    col = lax.broadcasted_iota(jnp.int32, (128, 128), 1)
    gap = row - col
    one, zero = jnp.float32(1.0), jnp.float32(0.0)
    same = jnp.where(jnp.abs(gap) <= SMOOTH, one, zero)
    before = jnp.where(gap >= SMOOTH, one, zero)
    after = jnp.where(gap <= -SMOOTH, one, zero)
    return jnp.concatenate([before, same, after], axis=0).astype(jnp.bfloat16)


def whiten_blocks(x_ref):
    fill = jnp.zeros((2, WIDTH), jnp.float32)
    re = jnp.concatenate([x_ref[:, 0, :].astype(jnp.float32), fill], axis=0)
    im = jnp.concatenate([x_ref[:, 1, :].astype(jnp.float32), fill], axis=0)
    blocks = WIDTH // 128

    def rows(value):
        return jnp.concatenate([value[:, 128 * k : 128 * k + 128] for k in range(blocks)], axis=0)

    re, im = rows(re), rows(im)
    amplitude = jnp.sqrt(re * re + im * im)
    high = amplitude.astype(jnp.bfloat16)
    low = (amplitude - high.astype(jnp.float32)).astype(jnp.bfloat16)
    weights = band()
    total = None
    for value in (high, low):
        value = value.astype(jnp.float32)
        edge = jnp.zeros((8, 128), jnp.float32)
        before = jnp.concatenate([edge, value[:-8]], axis=0)
        after = jnp.concatenate([value[8:], edge], axis=0)
        wide = jnp.concatenate([before, value, after], axis=1).astype(jnp.bfloat16)
        term = jnp.dot(wide, weights, preferred_element_type=jnp.float32)
        total = term if total is None else total + term
    row = lax.broadcasted_iota(jnp.int32, (128, 128), 0)
    col = lax.broadcasted_iota(jnp.int32, (128, 128), 1)
    position = (row // 8) * 128 + col
    lower = jnp.maximum(position - SMOOTH, 0)
    upper = jnp.minimum(position + SMOOTH, WIDTH - 1)
    bins = (upper - lower + 1).astype(jnp.float32)
    smoothed = total / bins
    scale = smoothed + epsilon
    return re / scale, im / scale


def station(x_at, z_at, core_at):
    return (x_at * NZ + z_at) * NC + core_at


def arrived(block, sem):
    pltpu.make_async_copy(block, block, sem).wait()


def kernel(x_hbm, pairs_ref, first_hbm, twiddle_hbm, out_ref,
           x_ref, first_ref, twiddle_ref, sent,
           flat, packed, every, left, swapped, lists, out_buf, daily, middle,
           const_sem, list_send, list_recv, one_send, one_recv, fwd_send, fwd_recv, day_send, day_recv, out_sem):
    y = lax.axis_index("tm")
    sta = lax.axis_index("sta")
    core = sta % NC
    column = sta // NC
    xx, zz = column // NZ, column % NZ
    chunks = (NC * y + core, NC * zz + core)

    def send(src, dst, send_sem, recv_sem, x_at, y_at, z_at, core_at):
        pltpu.make_async_remote_copy(
            src_ref=src,
            dst_ref=dst,
            send_sem=send_sem,
            recv_sem=recv_sem,
            device_id=(y_at, station(x_at, z_at, core_at)),
            device_id_type=MESH,
        ).start()

    load = pltpu.make_async_copy(x_hbm, x_ref, const_sem.at[0])
    load.start()
    barrier = pltpu.get_barrier_semaphore()
    greeted = 0
    for dx in (2, 1, 3, 0):
        for dy in (2, 1, 3, 0):
            for dz in (2, 1, 3, 0):
                if dx > 0 and dy > 0 and dz > 0:
                    continue
                for dc in range(NC):
                    if (dx, dy, dz, dc) == (0, 0, 0, 0):
                        continue
                    peer = station((xx + dx) % NX, (zz + dz) % NZ, (core + dc) % NC)
                    pl.semaphore_signal(
                        barrier, inc=1, device_id=((y + dy) % NY, peer), device_id_type=MESH
                    )
                    greeted += 1

    pltpu.make_async_copy(pairs_ref, lists.at[zz, core], list_recv.at[zz, core]).start()
    tables = [
        pltpu.make_async_copy(first_hbm, first_ref, const_sem.at[1]),
        pltpu.make_async_copy(twiddle_hbm, twiddle_ref, const_sem.at[2]),
    ]
    for table in tables:
        table.start()
    load.wait()

    white_re, white_im = whiten_blocks(x_ref)
    flat[0] = white_re
    flat[1] = white_im
    turned = []
    for row in range(SEGS * 3):
        pieces = []
        for part in range(2):
            tile = flat[part, pl.ds(row, 16, stride=8), :]
            for m in range(4):
                pieces.append(tile if m == 0 else pltpu.roll(tile, 128 - 32 * m, 1))
        stacked = jnp.concatenate(pieces, axis=0)
        turned.append(jnp.transpose(stacked, (1, 0))[:F2])
    for source in range(SOURCES):
        for comp in range(3):
            tile = jnp.concatenate(
                [turned[seg * 3 + comp][LOCAL * source : LOCAL * source + LOCAL] for seg in range(SEGS)],
                axis=0,
            )
            packed[source, comp] = tile.astype(jnp.bfloat16)

    pl.semaphore_wait(barrier, greeted)

    places = (xx * (1 - core) + zz * core, xx * (1 - core) + y * core)
    for dj, di in ((2, 2), (2, 1), (2, 3), (1, 2), (3, 2), (1, 1), (3, 3), (1, 3), (3, 1),
                   (2, 0), (0, 2), (1, 0), (3, 0), (0, 1), (0, 3), (0, 0)):
        for dc in range(NC):
            for bins in range(SETS):
                if (dj, di, dc) == (0, 0, 0):
                    continue
                core_at = (core + dc) % NC
                x_at = (xx + di * (1 - core)) % NX
                if bins == 0:
                    y_at, z_at = (y + dj) % NY, (zz + di * core) % NZ
                    chunk = NC * y_at + core_at
                else:
                    y_at, z_at = (y + di * core) % NY, (zz + dj) % NZ
                    chunk = NC * z_at + core_at
                send(packed.at[CHUNKS * bins + chunk], every.at[bins, xx, zz, core, y],
                     one_send, one_recv.at[bins, core, places[bins]], x_at, y_at, z_at, core_at)
    for bins in range(SETS):
        pltpu.make_async_copy(
            packed.at[CHUNKS * bins + chunks[bins]],
            every.at[bins, xx, zz, core, y],
            one_recv.at[bins, core, places[bins]],
        ).start()
    list_peers = [(dz, dc) for dz in (2, 1, 3, 0) for dc in range(NC) if (dz, dc) != (0, 0)]
    for at, (dz, dc) in enumerate(list_peers):
        send(pairs_ref, lists.at[zz, core], list_send.at[at], list_recv.at[zz, core],
             xx, y, (zz + dz) % NZ, (core + dc) % NC)

    lane = lax.broadcasted_iota(jnp.int32, (8, 128), 1)
    sub = lax.broadcasted_iota(jnp.int32, (8, 128), 0)
    is_re = lane < 64
    is_low = sub < 4
    is_even = (sub // 2) % 2 == 0
    sign = jnp.where(is_re, jnp.float32(-1.0), jnp.float32(1.0))

    def widen(bins, x_at, z_at, core_at):
        at = station(x_at, z_at, core_at)
        for pair in range(HOURS // 2):
            for comp in range(3):
                value = jnp.concatenate(
                    [every[bins, x_at, z_at, core_at, 2 * pair + hour, comp].astype(jnp.float32)
                     for hour in range(2)], axis=0
                )
                left[bins, at, pair, comp] = value
                swapped[bins, at, pair, comp] = pltpu.roll(value, 64, 1) * sign

    for d in (0, 1, 3, 2):
        for bins in range(SETS):
            for side in range(2):
                if side == 0:
                    spot = (xx + d) % NX
                    piece = every.at[0, spot, zz, 0] if bins == 0 else every.at[1, spot, :, 0, y]
                elif bins == 0:
                    spot = (zz + d) % NZ
                    piece = every.at[0, xx, spot, 1]
                else:
                    spot = (y + d) % NY
                    piece = every.at[1, xx, :, 1, spot]
                arrived(piece, one_recv.at[bins, side, spot])
                for to in (2, 1, 3):
                    if side == 1:
                        x_at, y_at, z_at, mine = (xx + to) % NX, y, zz, xx
                    elif bins == 0:
                        x_at, y_at, z_at, mine = xx, y, (zz + to) % NZ, zz
                    else:
                        x_at, y_at, z_at, mine = xx, (y + to) % NY, zz, y
                    send(piece, piece, fwd_send, fwd_recv.at[bins, side, mine], x_at, y_at, z_at, core)
    for d in range(4):
        widen(0, d, zz, 0)
        widen(0, xx, d, 1)
        widen(1, xx, d, 1)
    for to in (1, 3, 2):
        x_at, z_at, y_at = (xx + to) % NX, (zz + to) % NZ, (y + to) % NY
        arrived(every.at[0, :, z_at, 0], fwd_recv.at[0, 0, z_at])
        for d in range(4):
            widen(0, d, z_at, 0)
        for bins in range(SETS):
            arrived(every.at[bins, x_at, :, 1], fwd_recv.at[bins, 1, x_at])
            for d in range(4):
                widen(bins, x_at, d, 1)
        arrived(every.at[1, :, :, 0, y_at], fwd_recv.at[1, 0, y_at])
    for x_at in range(NX):
        for z_at in range(NZ):
            widen(1, x_at, z_at, 0)
    for z_at in range(NZ):
        for core_at in range(NC):
            arrived(lists.at[z_at, core_at], list_recv.at[z_at, core_at])

    def slot_products(bins, first, second):
        plain, crossed = [None] * 9, [None] * 9
        for pair in range(HOURS // 2):
            one = [left[bins, first, pair, comp] for comp in range(3)]
            turn = [swapped[bins, first, pair, comp] for comp in range(3)]
            two = [left[bins, second, pair, comp] for comp in range(3)]
            for a in range(3):
                for b in range(3):
                    at = 3 * a + b
                    p, q = one[a] * two[b], turn[a] * two[b]
                    plain[at] = p if pair == 0 else plain[at] + p
                    crossed[at] = q if pair == 0 else crossed[at] + q
        joined = []
        for at in range(9):
            keep = jnp.where(is_re, plain[at], crossed[at])
            move = jnp.where(is_re, crossed[at], plain[at])
            joined.append(keep + pltpu.roll(move, 64, 1))
        return joined

    def fold(one, two, mask, distance):
        keep = jnp.where(mask, one, two)
        move = jnp.where(mask, two, one)
        return keep + pltpu.roll(move, distance, 0)

    def fill(target, bins, z_at, core_at, first_slot):
        def make(slot, slots, tile):
            values = []
            for at in range(slots):
                values += slot_products(bins, lists[z_at, core_at, 0, slot + at], lists[z_at, core_at, 1, slot + at])
            values += values[-2:] * ((-len(values) % 4) // 2)
            for at in range(len(values) // 4):
                a, b, c, d = values[4 * at : 4 * at + 4]
                target[tile + at] = fold(
                    fold(a, b, is_even, 2), fold(c, d, is_even, 2), is_low, 4
                ).astype(jnp.bfloat16)

        def step(at, carry):
            make(first_slot + 4 * at, 4, 9 * at)
            return carry

        lax.fori_loop(0, SHARE // 4, step, 0)
        make(first_slot + SHARE // 4 * 4, SHARE % 4, SHARE // 4 * 9)

    offsets = ((2, 0), (2, 1), (1, 0), (1, 1), (3, 0), (3, 1), (0, 1))
    for at, (d, dc) in enumerate(offsets):
        for bins in range(SETS):
            core_at = (core + dc) % NC
            y_at, z_at = ((y + d) % NY, zz) if bins == 0 else (y, (zz + d) % NZ)
            fill(out_buf.at[bins, at], bins, z_at, core_at, SHARE * y_at)
            send(out_buf.at[bins, at], daily.at[bins, chunks[bins]], day_send,
                 day_recv.at[bins, chunks[bins]], xx, y_at, z_at, core_at)
    for bins in range(SETS):
        fill(daily.at[bins, chunks[bins]], bins, zz, core, SHARE * y)

    for table in tables:
        table.wait()

    def stage_one(bins, chunk):
        rows = daily[bins, chunk].astype(jnp.float32).reshape(TILES * 8, 128).astype(jnp.bfloat16)
        product = jnp.dot(rows, first_ref[...], preferred_element_type=jnp.float32)
        re = product[:, :128].reshape(TILES, 8, 128)
        im = product[:, 128:].reshape(TILES, 8, 128)
        source = CHUNKS * bins + chunk
        turn_re, turn_im = twiddle_ref[source, 0], twiddle_ref[source, 1]
        middle[source, 0] = (re * turn_re - im * turn_im).astype(jnp.bfloat16)
        middle[source, 1] = (re * turn_im + im * turn_re).astype(jnp.bfloat16)
        pltpu.make_async_copy(middle.at[source], out_ref.at[source], out_sem).start()

    for d, dc in ((0, 0), (0, 1), (2, 0), (2, 1), (1, 0), (1, 1), (3, 0), (3, 1)):
        for bins in range(SETS):
            at = (y if bins == 0 else zz) + 4 - d
            chunk = NC * (at % 4) + (core + dc) % NC
            if (d, dc) != (0, 0):
                arrived(daily.at[bins, chunk], day_recv.at[bins, chunk])
            stage_one(bins, chunk)

    arrived(middle, out_sem)
    for at in range(7):
        arrived(lists.at[0, 0], list_send.at[at])
    arrived(sent, one_send)
    arrived(every.at[:, pl.ds(0, 3)], fwd_send)
    arrived(out_buf, day_send)


def lags_kernel(count_ref, middle_hbm, second_hbm, out_ref, middle, second, staged, in_sem, second_sem, out_sem):
    first_slot = lax.axis_index("tm") * SHARE
    count = count_ref[0]
    table = pltpu.make_async_copy(second_hbm, second, second_sem)
    table.start()
    loads = []
    for at in range(len(CUTS) - 1):
        span = pl.ds(CUTS[at], CUTS[at + 1] - CUTS[at])
        load = pltpu.make_async_copy(middle_hbm.at[:, :, span], middle.at[:, :, span], in_sem.at[at])
        load.start()
        loads.append(load)
    table.wait()
    stores = []
    for at, load in enumerate(loads):
        load.wait()
        for group in range(3 * at, 3 * at + 3):
            tile = 3 * group // 2
            columns = jnp.concatenate(
                [middle[source, part, tile : tile + 2].astype(jnp.float32).reshape(16, 128)
                 for part in range(2) for source in range(SOURCES)], axis=0
            ).astype(jnp.bfloat16)
            total = jnp.dot(second[group % 2], columns, preferred_element_type=jnp.float32)
            for which in range(2):
                index = 2 * group + which
                live = first_slot + index // 3 < count
                for coarse in range(32):
                    start = 128 * which + 4 * coarse
                    value = total[start : start + 3]
                    value = jnp.where(live, value, jnp.zeros_like(value))
                    staged[index, :, 128 * coarse : 128 * coarse + 128] = value.astype(jnp.bfloat16)
        block = pl.ds(6 * at, 6)
        store = pltpu.make_async_copy(staged.at[block], out_ref.at[block], out_sem.at[at])
        store.start()
        stores.append(store)
    for store in stores:
        store.wait()


def body(spectra, pair_blocks, block_count):
    values = spectra.reshape(SEGS * 3, 2, WIDTH)
    pairs = pair_blocks[0].T
    first, twiddle, second = (jnp.asarray(value) for value in constants())
    f32, bf16 = jnp.float32, jnp.bfloat16
    anywhere = pl.BlockSpec(memory_space=pl.ANY)
    middle_shape = (SOURCES, 2, TILES, 8, 128)
    middle = pl.pallas_call(
        kernel,
        out_shape=jax.ShapeDtypeStruct(middle_shape, bf16),
        in_specs=[anywhere] * 4,
        out_specs=anywhere,
        scratch_shapes=[
            VMEM(values.shape, bf16),
            VMEM(first.shape, bf16),
            VMEM(twiddle.shape, f32),
            VMEM((31 * SETS, 3, ROWS, 128), bf16),
            VMEM((2, 128, 128), f32),
            VMEM((SOURCES, 3, ROWS, 128), bf16),
            VMEM((SETS, NX, NZ, NC, HOURS, 3, ROWS, 128), bf16),
            VMEM((SETS, STATIONS, HOURS // 2, 3, 8, 128), f32),
            VMEM((SETS, STATIONS, HOURS // 2, 3, 8, 128), f32),
            pltpu.SMEM((NZ, NC) + pairs.shape, jnp.int32),
            VMEM((SETS, 7, TILES, 8, 128), bf16),
            VMEM((SETS, CHUNKS, TILES, 8, 128), bf16),
            VMEM(middle_shape, bf16),
            DMA((3,)),
            DMA((7,)),
            DMA((NZ, NC)),
            DMA(()),
            DMA((SETS, 2, 4)),
            DMA(()),
            DMA((SETS, 2, 4)),
            DMA(()),
            DMA((SETS, CHUNKS)),
            DMA(()),
        ],
        compiler_params=pltpu.CompilerParams(collective_id=0, has_side_effects=True),
        name="correlate",
    )(values, pairs, first, twiddle)
    lags = pl.pallas_call(
        lags_kernel,
        out_shape=jax.ShapeDtypeStruct((SHARE * 3, 3, LAGS), bf16),
        in_specs=[pl.BlockSpec(memory_space=pltpu.SMEM), anywhere, anywhere],
        out_specs=anywhere,
        scratch_shapes=[
            VMEM(middle_shape, bf16),
            VMEM(second.shape, bf16),
            VMEM((SHARE * 3, 3, LAGS), bf16),
            DMA((len(CUTS) - 1,)),
            DMA(()),
            DMA((len(CUTS) - 1,)),
        ],
        name="lags",
    )(block_count, middle, second)
    return lags.reshape(1, SHARE, 1, 1, 3, 3, LAGS)


def solution(mesh):
    placed = (P("tm", "sta", None, None, None, None), P("sta", None, None), P("sta"))
    return jax.shard_map(
        body,
        mesh=mesh,
        in_specs=placed,
        out_specs=P("sta", "tm", None, None, None, None, None),
        check_vma=False,
    )
```

time: 36.9 us -> 34.9 us (0.946)
  Pallas kernels: 36 us -> 34 us
    pallas_call x2, Pallas kernels: 36 us -> 34 us  [the longest x1 30 us: body(): pl.pallas_call(kernel, out_shape=jax.ShapeDtypeStruct(middle_shape, bf16)...]
where the time goes in v3:
time: 34.9 us; the launch traced here: 34.7 us
  Pallas kernels  34 us (97%)
  between operations  0.66 us (2%)
    pallas_call x1, Pallas kernels, body(): pl.pallas_call(kernel, out_shape=jax.ShapeDtypeStruct(middle_shape, bf16)...  30 us
    pallas_call x1, Pallas kernels, body(): pl.pallas_call(lags_kernel, out_shape=jax.ShapeDtypeStruct((SHARE * 3, 3,...  3.99 us

profile of v3, /device:TPU:1, one launch (start us, length us, event | category | flops | bytes accessed | tf_op | source)
XLA Modules:
  0.0 34.7 jit_solution(4607101415219491903)
XLA Ops:
  0.7 30.0 %correlate.1.middle_hbm = bf16[16,2,23,8,128]{4,3,2,1,0:T(8,128)(2,1)} custom-call(bf16[6,2,2048]{2,1,0:T(2,128)(2,1)} %bitcast.7, s32[2,40]{1,0:T(2,128)} %bitcast.8, bf16[128,256]{1,0:T(8,128)(2,1)} %constant.6.clone.first_hbm, f32[16,2,8,128]{3,2,1,0:T(8,128)} %constant.7.clone.twiddle_hbm), custom_call_target="tpu_custom_call" | custom-call | tf_op jit(solution)/shard_map/correlate/pallas_call | solution.py:410
  30.7 4.0 %lags.1 = bf16[30,3,4096]{2,1,0:T(4,128)(2,1)} custom-call(s32[1]{0:T(128)S(6)} %copy.8.count_ref, bf16[16,2,23,8,128]{4,3,2,1,0:T(8,128)(2,1)} %correlate.1.middle_hbm, bf16[2,256,512]{2,1,0:T(8,128)(2,1)} %constant.8.clone.second_hbm), custom_call_target="tpu_custom_call" | custom-call | tf_op jit(solution)/shard_map/lags/pallas_call | solution.py:443

commit v4 on v3

--- a/solution.py
+++ b/solution.py
@@ -31,7 +31,7 @@
 SHARE = 10
 TILES = -(-SHARE * 9 * LOCAL // 8)
 GROUPS = SHARE * 3 // 2
-CUTS = (0, 5, 9, 14, 18, 23)
+CUTS = (0, 3, 6, 9, 12, 14, 15)
 
 
 def constants():
@@ -120,10 +120,10 @@
     pltpu.make_async_copy(block, block, sem).wait()
 
 
-def kernel(x_hbm, pairs_ref, first_hbm, twiddle_hbm, out_ref,
+def kernel(x_hbm, pairs_ref, first_hbm, twiddle_hbm, middle,
            x_ref, first_ref, twiddle_ref, sent,
-           flat, packed, every, left, swapped, lists, out_buf, daily, middle,
-           const_sem, list_send, list_recv, one_send, one_recv, fwd_send, fwd_recv, day_send, day_recv, out_sem):
+           flat, packed, every, left, swapped, lists, out_buf, daily,
+           const_sem, list_send, list_recv, one_send, one_recv, fwd_send, fwd_recv, day_send, day_recv):
     y = lax.axis_index("tm")
     sta = lax.axis_index("sta")
     core = sta % NC
@@ -190,7 +190,14 @@
 
     pl.semaphore_wait(barrier, greeted)
 
-    places = (xx * (1 - core) + zz * core, xx * (1 - core) + y * core)
+    scatter, across = (y, zz), (zz, y)
+    spots = tuple(NY * core + s_at for s_at in scatter)
+    parts = tuple(core * ((s_at + 3) // 4) for s_at in scatter)
+    places = tuple(xx * (1 - p) + w_at * p for p, w_at in zip(parts, across))
+
+    def at_axes(bins, s_at, w_at):
+        return (s_at, w_at) if bins == 0 else (w_at, s_at)
+
     for dj, di in ((2, 2), (2, 1), (2, 3), (1, 2), (3, 2), (1, 1), (3, 3), (1, 3), (3, 1),
                    (2, 0), (0, 2), (1, 0), (3, 0), (0, 1), (0, 3), (0, 0)):
         for dc in range(NC):
@@ -198,20 +205,17 @@
                 if (dj, di, dc) == (0, 0, 0):
                     continue
                 core_at = (core + dc) % NC
-                x_at = (xx + di * (1 - core)) % NX
-                if bins == 0:
-                    y_at, z_at = (y + dj) % NY, (zz + di * core) % NZ
-                    chunk = NC * y_at + core_at
-                else:
-                    y_at, z_at = (y + di * core) % NY, (zz + dj) % NZ
-                    chunk = NC * z_at + core_at
-                send(packed.at[CHUNKS * bins + chunk], every.at[bins, xx, zz, core, y],
-                     one_send, one_recv.at[bins, core, places[bins]], x_at, y_at, z_at, core_at)
+                s_at = (scatter[bins] + dj) % 4
+                x_at = (xx + di * (1 - parts[bins])) % NX
+                w_at = (across[bins] + di * parts[bins]) % 4
+                y_at, z_at = at_axes(bins, s_at, w_at)
+                send(packed.at[CHUNKS * bins + NC * s_at + core_at], every.at[bins, xx, across[bins], spots[bins]],
+                     one_send, one_recv.at[bins, parts[bins], places[bins]], x_at, y_at, z_at, core_at)
     for bins in range(SETS):
         pltpu.make_async_copy(
             packed.at[CHUNKS * bins + chunks[bins]],
-            every.at[bins, xx, zz, core, y],
-            one_recv.at[bins, core, places[bins]],
+            every.at[bins, xx, across[bins], spots[bins]],
+            one_recv.at[bins, parts[bins], places[bins]],
         ).start()
     list_peers = [(dz, dc) for dz in (2, 1, 3, 0) for dc in range(NC) if (dz, dc) != (0, 0)]
     for at, (dz, dc) in enumerate(list_peers):
@@ -229,51 +233,57 @@
         at = station(x_at, z_at, core_at)
         for pair in range(HOURS // 2):
             for comp in range(3):
-                value = jnp.concatenate(
-                    [every[bins, x_at, z_at, core_at, 2 * pair + hour, comp].astype(jnp.float32)
-                     for hour in range(2)], axis=0
-                )
+                hours = (2 * pair, 2 * pair + 1)
+                if bins == 0:
+                    halves = [every[0, x_at, z_at, NY * core_at + hour, comp] for hour in hours]
+                else:
+                    halves = [every[1, x_at, hour, NZ * core_at + z_at, comp] for hour in hours]
+                value = jnp.concatenate([half.astype(jnp.float32) for half in halves], axis=0)
                 left[bins, at, pair, comp] = value
                 swapped[bins, at, pair, comp] = pltpu.roll(value, 64, 1) * sign
 
+    split = (pl.ds(0, 5), pl.ds(5, 3))
     for d in (0, 1, 3, 2):
         for bins in range(SETS):
-            for side in range(2):
-                if side == 0:
+            for part in range(2):
+                if part == 0:
                     spot = (xx + d) % NX
-                    piece = every.at[0, spot, zz, 0] if bins == 0 else every.at[1, spot, :, 0, y]
-                elif bins == 0:
-                    spot = (zz + d) % NZ
-                    piece = every.at[0, xx, spot, 1]
+                    piece = every.at[bins, spot, across[bins], split[0]]
                 else:
-                    spot = (y + d) % NY
-                    piece = every.at[1, xx, :, 1, spot]
-                arrived(piece, one_recv.at[bins, side, spot])
+                    spot = (across[bins] + d) % 4
+                    piece = every.at[bins, xx, spot, split[1]]
+                arrived(piece, one_recv.at[bins, part, spot])
                 for to in (2, 1, 3):
-                    if side == 1:
+                    if part == 1:
                         x_at, y_at, z_at, mine = (xx + to) % NX, y, zz, xx
-                    elif bins == 0:
-                        x_at, y_at, z_at, mine = xx, y, (zz + to) % NZ, zz
                     else:
-                        x_at, y_at, z_at, mine = xx, (y + to) % NY, zz, y
-                    send(piece, piece, fwd_send, fwd_recv.at[bins, side, mine], x_at, y_at, z_at, core)
+                        y_at, z_at = at_axes(bins, scatter[bins], (across[bins] + to) % 4)
+                        x_at, mine = xx, across[bins]
+                    send(piece, piece, fwd_send, fwd_recv.at[bins, part, mine], x_at, y_at, z_at, core)
     for d in range(4):
         widen(0, d, zz, 0)
-        widen(0, xx, d, 1)
-        widen(1, xx, d, 1)
+        if d > 0:
+            widen(1, xx, d, 1)
     for to in (1, 3, 2):
-        x_at, z_at, y_at = (xx + to) % NX, (zz + to) % NZ, (y + to) % NY
-        arrived(every.at[0, :, z_at, 0], fwd_recv.at[0, 0, z_at])
+        z_at = (zz + to) % NZ
+        arrived(every.at[0, :, z_at, split[0]], fwd_recv.at[0, 0, z_at])
         for d in range(4):
             widen(0, d, z_at, 0)
+    for d in range(4):
+        widen(0, xx, d, 1)
+    for to in (1, 3, 2):
+        x_at = (xx + to) % NX
         for bins in range(SETS):
-            arrived(every.at[bins, x_at, :, 1], fwd_recv.at[bins, 1, x_at])
-            for d in range(4):
+            arrived(every.at[bins, x_at, :, split[1]], fwd_recv.at[bins, 1, x_at])
+            for d in range(bins, 4):
                 widen(bins, x_at, d, 1)
-        arrived(every.at[1, :, :, 0, y_at], fwd_recv.at[1, 0, y_at])
+    for to in (1, 3, 2):
+        y_at = (y + to) % NY
+        arrived(every.at[1, :, y_at, split[0]], fwd_recv.at[1, 0, y_at])
     for x_at in range(NX):
         for z_at in range(NZ):
             widen(1, x_at, z_at, 0)
+        widen(1, x_at, 0, 1)
     for z_at in range(NZ):
         for core_at in range(NC):
             arrived(lists.at[z_at, core_at], list_recv.at[z_at, core_at])
@@ -344,7 +354,6 @@
         turn_re, turn_im = twiddle_ref[source, 0], twiddle_ref[source, 1]
         middle[source, 0] = (re * turn_re - im * turn_im).astype(jnp.bfloat16)
         middle[source, 1] = (re * turn_im + im * turn_re).astype(jnp.bfloat16)
-        pltpu.make_async_copy(middle.at[source], out_ref.at[source], out_sem).start()
 
     for d, dc in ((0, 0), (0, 1), (2, 0), (2, 1), (1, 0), (1, 1), (3, 0), (3, 1)):
         for bins in range(SETS):
@@ -354,7 +363,6 @@
                 arrived(daily.at[bins, chunk], day_recv.at[bins, chunk])
             stage_one(bins, chunk)
 
-    arrived(middle, out_sem)
     for at in range(7):
         arrived(lists.at[0, 0], list_send.at[at])
     arrived(sent, one_send)
@@ -362,22 +370,12 @@
     arrived(out_buf, day_send)
 
 
-def lags_kernel(count_ref, middle_hbm, second_hbm, out_ref, middle, second, staged, in_sem, second_sem, out_sem):
+def lags_kernel(count_ref, middle, second, out_ref, staged, out_sem):
     first_slot = lax.axis_index("tm") * SHARE
     count = count_ref[0]
-    table = pltpu.make_async_copy(second_hbm, second, second_sem)
-    table.start()
-    loads = []
-    for at in range(len(CUTS) - 1):
-        span = pl.ds(CUTS[at], CUTS[at + 1] - CUTS[at])
-        load = pltpu.make_async_copy(middle_hbm.at[:, :, span], middle.at[:, :, span], in_sem.at[at])
-        load.start()
-        loads.append(load)
-    table.wait()
     stores = []
-    for at, load in enumerate(loads):
-        load.wait()
-        for group in range(3 * at, 3 * at + 3):
+    for at, (begin, end) in enumerate(zip(CUTS, CUTS[1:])):
+        for group in range(begin, end):
             tile = 3 * group // 2
             columns = jnp.concatenate(
                 [middle[source, part, tile : tile + 2].astype(jnp.float32).reshape(16, 128)
@@ -392,7 +390,7 @@
                     value = total[start : start + 3]
                     value = jnp.where(live, value, jnp.zeros_like(value))
                     staged[index, :, 128 * coarse : 128 * coarse + 128] = value.astype(jnp.bfloat16)
-        block = pl.ds(6 * at, 6)
+        block = pl.ds(2 * begin, 2 * (end - begin))
         store = pltpu.make_async_copy(staged.at[block], out_ref.at[block], out_sem.at[at])
         store.start()
         stores.append(store)
@@ -407,11 +405,12 @@
     f32, bf16 = jnp.float32, jnp.bfloat16
     anywhere = pl.BlockSpec(memory_space=pl.ANY)
     middle_shape = (SOURCES, 2, TILES, 8, 128)
+    in_vmem = pl.BlockSpec(memory_space=pltpu.VMEM)
     middle = pl.pallas_call(
         kernel,
         out_shape=jax.ShapeDtypeStruct(middle_shape, bf16),
-        in_specs=[anywhere] * 4,
-        out_specs=anywhere,
+        in_specs=[pl.BlockSpec(memory_space=pltpu.HBM)] * 4,
+        out_specs=in_vmem,
         scratch_shapes=[
             VMEM(values.shape, bf16),
             VMEM(first.shape, bf16),
@@ -419,13 +418,12 @@
             VMEM((31 * SETS, 3, ROWS, 128), bf16),
             VMEM((2, 128, 128), f32),
             VMEM((SOURCES, 3, ROWS, 128), bf16),
-            VMEM((SETS, NX, NZ, NC, HOURS, 3, ROWS, 128), bf16),
+            VMEM((SETS, NX, 4, NC * 4, 3, ROWS, 128), bf16),
             VMEM((SETS, STATIONS, HOURS // 2, 3, 8, 128), f32),
             VMEM((SETS, STATIONS, HOURS // 2, 3, 8, 128), f32),
             pltpu.SMEM((NZ, NC) + pairs.shape, jnp.int32),
             VMEM((SETS, 7, TILES, 8, 128), bf16),
             VMEM((SETS, CHUNKS, TILES, 8, 128), bf16),
-            VMEM(middle_shape, bf16),
             DMA((3,)),
             DMA((7,)),
             DMA((NZ, NC)),
@@ -435,24 +433,22 @@
             DMA((SETS, 2, 4)),
             DMA(()),
             DMA((SETS, CHUNKS)),
-            DMA(()),
         ],
-        compiler_params=pltpu.CompilerParams(collective_id=0, has_side_effects=True),
+        compiler_params=pltpu.CompilerParams(
+            collective_id=0, has_side_effects=True, vmem_limit_bytes=24 << 20
+        ),
         name="correlate",
-    )(values, pairs, first, twiddle)
+    )(*(pltpu.with_memory_space_constraint(value, pltpu.HBM) for value in (values, pairs, first, twiddle)))
     lags = pl.pallas_call(
         lags_kernel,
         out_shape=jax.ShapeDtypeStruct((SHARE * 3, 3, LAGS), bf16),
-        in_specs=[pl.BlockSpec(memory_space=pltpu.SMEM), anywhere, anywhere],
+        in_specs=[pl.BlockSpec(memory_space=pltpu.SMEM), in_vmem, in_vmem],
         out_specs=anywhere,
         scratch_shapes=[
-            VMEM(middle_shape, bf16),
-            VMEM(second.shape, bf16),
             VMEM((SHARE * 3, 3, LAGS), bf16),
             DMA((len(CUTS) - 1,)),
-            DMA(()),
-            DMA((len(CUTS) - 1,)),
         ],
+        compiler_params=pltpu.CompilerParams(vmem_limit_bytes=16 << 20),
         name="lags",
     )(block_count, middle, second)
     return lags.reshape(1, SHARE, 1, 1, 3, 3, LAGS)

time: 34.9 us -> 31.2 us (0.89)
  Pallas kernels: 34 us -> 30.3 us
    pallas_call x1, Pallas kernels: 3.99 us -> 1.86 us  [body(): pl.pallas_call(lags_kernel, out_shape=jax.ShapeDtypeStruct((SHARE * 3, 3,...]
    pallas_call x1, Pallas kernels: 30 us -> 28.4 us  [body(): pl.pallas_call(kernel, out_shape=jax.ShapeDtypeStruct(middle_shape, bf16)...]
where the time goes in v4:
time: 31.2 us; the launch traced here: 31 us
  Pallas kernels  30.3 us (97%)
  between operations  0.73 us (2%)
    pallas_call x1, Pallas kernels, body(): pl.pallas_call(kernel, out_shape=jax.ShapeDtypeStruct(middle_shape, bf16)...  28.4 us
    pallas_call x1, Pallas kernels, body(): pl.pallas_call(lags_kernel, out_shape=jax.ShapeDtypeStruct((SHARE * 3, 3,...  1.86 us

profile of v4, /device:TPU:1, one launch (start us, length us, event | category | flops | bytes accessed | tf_op | source)
XLA Modules:
  0.0 31.0 jit_solution(3608230855250447733)
XLA Ops:
  0.0 0.0 copy-start
  0.7 28.4 %correlate.1.middle = bf16[16,2,23,8,128]{4,3,2,1,0:T(8,128)(2,1)S(1)} custom-call(bf16[6,2,2048]{2,1,0:T(2,128)(2,1)} %bitcast.7, s32[2,40]{1,0:T(2,128)} %bitcast.8, bf16[128,256]{1,0:T(8,128)(2,1)} %constant.6.clone.first_hbm, f32[16,2,8,128]{3,2,1,0:T(8,128)} %constant.7.clone.twiddle_hbm), custom_call_target="tpu_custom_call" | custom-call | tf_op jit(solution)/shard_map/correlate/pallas_call | solution.py:409
  29.2 0.0 copy-done
  29.2 1.9 %lags.1 = bf16[30,3,4096]{2,1,0:T(4,128)(2,1)} custom-call(s32[1]{0:T(128)S(6)} %copy.8.count_ref, bf16[16,2,23,8,128]{4,3,2,1,0:T(8,128)(2,1)S(1)} %correlate.1.middle, bf16[2,256,512]{2,1,0:T(8,128)(2,1)S(1)} %copy-done), custom_call_target="tpu_custom_call" | custom-call | tf_op jit(solution)/shard_map/lags/pallas_call | solution.py:442
Async XLA Ops:
  0.0 29.2 %copy-start = (bf16[2,256,512]{2,1,0:T(8,128)(2,1)S(1)}, bf16[2,256,512]{2,1,0:T(8,128)(2,1)}, u32[]{:S(2)}) copy-start(bf16[2,256,512]{2,1,0:T(8,128)(2,1)} %constant.8.clone.second) | copy-start | bytes 1572868

commit v5 on v4

--- a/solution.py
+++ b/solution.py
@@ -32,6 +32,11 @@
 TILES = -(-SHARE * 9 * LOCAL // 8)
 GROUPS = SHARE * 3 // 2
 CUTS = (0, 3, 6, 9, 12, 14, 15)
+
+
+GREETED = sorted(
+    [d for d in np.ndindex(NX, NY, NZ) if 0 in d], key=lambda d: -sum(min(at, 4 - at) for at in d)
+)
 
 
 def constants():
@@ -145,19 +150,13 @@
     load.start()
     barrier = pltpu.get_barrier_semaphore()
     greeted = 0
-    for dx in (2, 1, 3, 0):
-        for dy in (2, 1, 3, 0):
-            for dz in (2, 1, 3, 0):
-                if dx > 0 and dy > 0 and dz > 0:
-                    continue
-                for dc in range(NC):
-                    if (dx, dy, dz, dc) == (0, 0, 0, 0):
-                        continue
-                    peer = station((xx + dx) % NX, (zz + dz) % NZ, (core + dc) % NC)
-                    pl.semaphore_signal(
-                        barrier, inc=1, device_id=((y + dy) % NY, peer), device_id_type=MESH
-                    )
-                    greeted += 1
+    for dx, dy, dz in GREETED:
+        for dc in range(NC):
+            if (dx, dy, dz, dc) == (0, 0, 0, 0):
+                continue
+            peer = station((xx + dx) % NX, (zz + dz) % NZ, (core + dc) % NC)
+            pl.semaphore_signal(barrier, inc=1, device_id=((y + dy) % NY, peer), device_id_type=MESH)
+            greeted += 1
 
     pltpu.make_async_copy(pairs_ref, lists.at[zz, core], list_recv.at[zz, core]).start()
     tables = [
@@ -331,7 +330,7 @@
         lax.fori_loop(0, SHARE // 4, step, 0)
         make(first_slot + SHARE // 4 * 4, SHARE % 4, SHARE // 4 * 9)
 
-    offsets = ((2, 0), (2, 1), (1, 0), (1, 1), (3, 0), (3, 1), (0, 1))
+    offsets = ((2, 0), (1, 0), (3, 0), (2, 1), (1, 1), (3, 1), (0, 1))
     for at, (d, dc) in enumerate(offsets):
         for bins in range(SETS):
             core_at = (core + dc) % NC
@@ -346,7 +345,7 @@
         table.wait()
 
     def stage_one(bins, chunk):
-        rows = daily[bins, chunk].astype(jnp.float32).reshape(TILES * 8, 128).astype(jnp.bfloat16)
+        rows = daily[bins, chunk].reshape(TILES * 8, 128)
         product = jnp.dot(rows, first_ref[...], preferred_element_type=jnp.float32)
         re = product[:, :128].reshape(TILES, 8, 128)
         im = product[:, 128:].reshape(TILES, 8, 128)
@@ -355,12 +354,16 @@
         middle[source, 0] = (re * turn_re - im * turn_im).astype(jnp.bfloat16)
         middle[source, 1] = (re * turn_im + im * turn_re).astype(jnp.bfloat16)
 
-    for d, dc in ((0, 0), (0, 1), (2, 0), (2, 1), (1, 0), (1, 1), (3, 0), (3, 1)):
-        for bins in range(SETS):
-            at = (y if bins == 0 else zz) + 4 - d
-            chunk = NC * (at % 4) + (core + dc) % NC
-            if (d, dc) != (0, 0):
-                arrived(daily.at[bins, chunk], day_recv.at[bins, chunk])
+    for batch in (((0, 0), (2, 0)), ((1, 0), (3, 0)), ((0, 1), (2, 1)), ((1, 1), (3, 1))):
+        ready = []
+        for d, dc in batch:
+            for bins in range(SETS):
+                at = (y if bins == 0 else zz) + 4 - d
+                chunk = NC * (at % 4) + (core + dc) % NC
+                if (d, dc) != (0, 0):
+                    arrived(daily.at[bins, chunk], day_recv.at[bins, chunk])
+                ready.append((bins, chunk))
+        for bins, chunk in ready:
             stage_one(bins, chunk)
 
     for at in range(7):

time: 31.2 us -> 30 us (0.962)
  Pallas kernels: 30.3 us -> 29.1 us
    pallas_call x1, Pallas kernels: 28.4 us -> 27.3 us  [body(): pl.pallas_call(kernel, out_shape=jax.ShapeDtypeStruct(middle_shape, bf16)...]
where the time goes in v5:
time: 30 us; the launch traced here: 29.8 us
  Pallas kernels  29.1 us (97%)
  between operations  0.73 us (2%)
    pallas_call x1, Pallas kernels, body(): pl.pallas_call(kernel, out_shape=jax.ShapeDtypeStruct(middle_shape, bf16)...  27.3 us
    pallas_call x1, Pallas kernels, body(): pl.pallas_call(lags_kernel, out_shape=jax.ShapeDtypeStruct((SHARE * 3, 3,...  1.86 us

profile of v5, /device:TPU:1, one launch (start us, length us, event | category | flops | bytes accessed | tf_op | source)
XLA Modules:
  0.0 29.8 jit_solution(10509100591961015266)
XLA Ops:
  0.0 0.0 copy-start
  0.7 27.3 %correlate.1.middle = bf16[16,2,23,8,128]{4,3,2,1,0:T(8,128)(2,1)S(1)} custom-call(bf16[6,2,2048]{2,1,0:T(2,128)(2,1)} %bitcast.7, s32[2,40]{1,0:T(2,128)} %bitcast.8, bf16[128,256]{1,0:T(8,128)(2,1)} %constant.6.clone.first_hbm, f32[16,2,8,128]{3,2,1,0:T(8,128)} %constant.7.clone.twiddle_hbm), custom_call_target="tpu_custom_call" | custom-call | tf_op jit(solution)/shard_map/correlate/pallas_call | solution.py:412
  28.0 0.0 copy-done
  28.0 1.9 %lags.1 = bf16[30,3,4096]{2,1,0:T(4,128)(2,1)} custom-call(s32[1]{0:T(128)S(6)} %copy.8.count_ref, bf16[16,2,23,8,128]{4,3,2,1,0:T(8,128)(2,1)S(1)} %correlate.1.middle, bf16[2,256,512]{2,1,0:T(8,128)(2,1)S(1)} %copy-done), custom_call_target="tpu_custom_call" | custom-call | tf_op jit(solution)/shard_map/lags/pallas_call | solution.py:445
Async XLA Ops:
  0.0 28.0 %copy-start = (bf16[2,256,512]{2,1,0:T(8,128)(2,1)S(1)}, bf16[2,256,512]{2,1,0:T(8,128)(2,1)}, u32[]{:S(2)}) copy-start(bf16[2,256,512]{2,1,0:T(8,128)(2,1)} %constant.8.clone.second) | copy-start | bytes 1572868

commit v6 on v5

--- a/solution.py
+++ b/solution.py
@@ -31,7 +31,7 @@
 SHARE = 10
 TILES = -(-SHARE * 9 * LOCAL // 8)
 GROUPS = SHARE * 3 // 2
-CUTS = (0, 3, 6, 9, 12, 14, 15)
+CUTS = (0, 4, 8, 12, 15)
 
 
 GREETED = sorted(
@@ -323,11 +323,8 @@
                     fold(a, b, is_even, 2), fold(c, d, is_even, 2), is_low, 4
                 ).astype(jnp.bfloat16)
 
-        def step(at, carry):
+        for at in range(SHARE // 4):
             make(first_slot + 4 * at, 4, 9 * at)
-            return carry
-
-        lax.fori_loop(0, SHARE // 4, step, 0)
         make(first_slot + SHARE // 4 * 4, SHARE % 4, SHARE // 4 * 9)
 
     offsets = ((2, 0), (1, 0), (3, 0), (2, 1), (1, 1), (3, 1), (0, 1))
@@ -378,21 +375,27 @@
     count = count_ref[0]
     stores = []
     for at, (begin, end) in enumerate(zip(CUTS, CUTS[1:])):
-        for group in range(begin, end):
-            tile = 3 * group // 2
-            columns = jnp.concatenate(
-                [middle[source, part, tile : tile + 2].astype(jnp.float32).reshape(16, 128)
-                 for part in range(2) for source in range(SOURCES)], axis=0
-            ).astype(jnp.bfloat16)
-            total = jnp.dot(second[group % 2], columns, preferred_element_type=jnp.float32)
-            for which in range(2):
-                index = 2 * group + which
-                live = first_slot + index // 3 < count
-                for coarse in range(32):
-                    start = 128 * which + 4 * coarse
-                    value = total[start : start + 3]
-                    value = jnp.where(live, value, jnp.zeros_like(value))
-                    staged[index, :, 128 * coarse : 128 * coarse + 128] = value.astype(jnp.bfloat16)
+        for odd in (1, 0):
+            groups = range(begin + odd, end, 2)
+            columns = []
+            for group in groups:
+                tile = 3 * group // 2
+                columns.append(jnp.concatenate(
+                    [middle[source, part, tile : tile + 2].astype(jnp.float32).reshape(16, 128)
+                     for part in range(2) for source in range(SOURCES)], axis=0
+                ).astype(jnp.bfloat16))
+            totals = jnp.dot(
+                second[odd], jnp.concatenate(columns, axis=1), preferred_element_type=jnp.float32
+            )
+            for side, group in enumerate(groups):
+                for which in range(2):
+                    index = 2 * group + which
+                    live = first_slot + index // 3 < count
+                    for coarse in range(32):
+                        start = 128 * which + 4 * coarse
+                        value = totals[start : start + 3, 128 * side : 128 * side + 128]
+                        value = jnp.where(live, value, jnp.zeros_like(value))
+                        staged[index, :, 128 * coarse : 128 * coarse + 128] = value.astype(jnp.bfloat16)
         block = pl.ds(2 * begin, 2 * (end - begin))
         store = pltpu.make_async_copy(staged.at[block], out_ref.at[block], out_sem.at[at])
         store.start()

time: 30 us -> 29.2 us (0.973)
  Pallas kernels: 29.1 us -> 28.3 us
    pallas_call x1, Pallas kernels: 27.3 us -> 26.7 us  [body(): pl.pallas_call(kernel, out_shape=jax.ShapeDtypeStruct(middle_shape, bf16)...]
where the time goes in v6:
time: 29.2 us; the launch traced here: 29 us
  Pallas kernels  28.3 us (97%)
  between operations  0.73 us (2%)
    pallas_call x1, Pallas kernels, body(): pl.pallas_call(kernel, out_shape=jax.ShapeDtypeStruct(middle_shape, bf16)...  26.7 us
    pallas_call x1, Pallas kernels, body(): pl.pallas_call(lags_kernel, out_shape=jax.ShapeDtypeStruct((SHARE * 3, 3,...  1.63 us

profile of v6, /device:TPU:1, one launch (start us, length us, event | category | flops | bytes accessed | tf_op | source)
XLA Modules:
  0.0 29.0 jit_solution(12200554958302554106)
XLA Ops:
  0.0 0.0 copy-start
  0.7 26.7 %correlate.1.middle = bf16[16,2,23,8,128]{4,3,2,1,0:T(8,128)(2,1)S(1)} custom-call(bf16[6,2,2048]{2,1,0:T(2,128)(2,1)} %bitcast.7, s32[2,40]{1,0:T(2,128)} %bitcast.8, bf16[128,256]{1,0:T(8,128)(2,1)} %constant.6.clone.first_hbm, f32[16,2,8,128]{3,2,1,0:T(8,128)} %constant.7.clone.twiddle_hbm), custom_call_target="tpu_custom_call" | custom-call | tf_op jit(solution)/shard_map/correlate/pallas_call | solution.py:415
  27.4 0.0 copy-done
  27.4 1.6 %lags.1 = bf16[30,3,4096]{2,1,0:T(4,128)(2,1)} custom-call(s32[1]{0:T(128)S(6)} %copy.8.count_ref, bf16[16,2,23,8,128]{4,3,2,1,0:T(8,128)(2,1)S(1)} %correlate.1.middle, bf16[2,256,512]{2,1,0:T(8,128)(2,1)S(1)} %copy-done), custom_call_target="tpu_custom_call" | custom-call | tf_op jit(solution)/shard_map/lags/pallas_call | solution.py:448
Async XLA Ops:
  0.0 27.4 %copy-start = (bf16[2,256,512]{2,1,0:T(8,128)(2,1)S(1)}, bf16[2,256,512]{2,1,0:T(8,128)(2,1)}, u32[]{:S(2)}) copy-start(bf16[2,256,512]{2,1,0:T(8,128)(2,1)} %constant.8.clone.second) | copy-start | bytes 1572868

commit v7 on v6

--- a/solution.py
+++ b/solution.py
@@ -228,14 +228,15 @@
     is_even = (sub // 2) % 2 == 0
     sign = jnp.where(is_re, jnp.float32(-1.0), jnp.float32(1.0))
 
-    def widen(bins, x_at, z_at, core_at):
+    def widen(bins, x_at, z_at, core_at, pairs=(0, 1)):
         at = station(x_at, z_at, core_at)
-        for pair in range(HOURS // 2):
+        for pair in pairs:
             for comp in range(3):
                 hours = (2 * pair, 2 * pair + 1)
                 if bins == 0:
                     halves = [every[0, x_at, z_at, NY * core_at + hour, comp] for hour in hours]
                 else:
+                    hours = [(y + hour) % HOURS for hour in hours]
                     halves = [every[1, x_at, hour, NZ * core_at + z_at, comp] for hour in hours]
                 value = jnp.concatenate([half.astype(jnp.float32) for half in halves], axis=0)
                 left[bins, at, pair, comp] = value
@@ -276,13 +277,14 @@
             arrived(every.at[bins, x_at, :, split[1]], fwd_recv.at[bins, 1, x_at])
             for d in range(bins, 4):
                 widen(bins, x_at, d, 1)
-    for to in (1, 3, 2):
-        y_at = (y + to) % NY
-        arrived(every.at[1, :, y_at, split[0]], fwd_recv.at[1, 0, y_at])
-    for x_at in range(NX):
-        for z_at in range(NZ):
-            widen(1, x_at, z_at, 0)
-        widen(1, x_at, 0, 1)
+    for pair, late in ((0, (1,)), (1, (3, 2))):
+        for to in late:
+            y_at = (y + to) % NY
+            arrived(every.at[1, :, y_at, split[0]], fwd_recv.at[1, 0, y_at])
+        for x_at in range(NX):
+            for z_at in range(NZ):
+                widen(1, x_at, z_at, 0, (pair,))
+            widen(1, x_at, 0, 1, (pair,))
     for z_at in range(NZ):
         for core_at in range(NC):
             arrived(lists.at[z_at, core_at], list_recv.at[z_at, core_at])
@@ -328,13 +330,15 @@
         make(first_slot + SHARE // 4 * 4, SHARE % 4, SHARE // 4 * 9)
 
     offsets = ((2, 0), (1, 0), (3, 0), (2, 1), (1, 1), (3, 1), (0, 1))
+    batches = (((0, 0), (2, 0)), ((1, 0), (3, 0)), ((0, 1), (2, 1)), ((1, 1), (3, 1)))
+    batch_of = {offset: at for at, batch in enumerate(batches) for offset in batch}
     for at, (d, dc) in enumerate(offsets):
         for bins in range(SETS):
             core_at = (core + dc) % NC
             y_at, z_at = ((y + d) % NY, zz) if bins == 0 else (y, (zz + d) % NZ)
             fill(out_buf.at[bins, at], bins, z_at, core_at, SHARE * y_at)
             send(out_buf.at[bins, at], daily.at[bins, chunks[bins]], day_send,
-                 day_recv.at[bins, chunks[bins]], xx, y_at, z_at, core_at)
+                 day_recv.at[batch_of[d, dc]], xx, y_at, z_at, core_at)
     for bins in range(SETS):
         fill(daily.at[bins, chunks[bins]], bins, zz, core, SHARE * y)
 
@@ -351,15 +355,13 @@
         middle[source, 0] = (re * turn_re - im * turn_im).astype(jnp.bfloat16)
         middle[source, 1] = (re * turn_im + im * turn_re).astype(jnp.bfloat16)
 
-    for batch in (((0, 0), (2, 0)), ((1, 0), (3, 0)), ((0, 1), (2, 1)), ((1, 1), (3, 1))):
-        ready = []
-        for d, dc in batch:
-            for bins in range(SETS):
-                at = (y if bins == 0 else zz) + 4 - d
-                chunk = NC * (at % 4) + (core + dc) % NC
-                if (d, dc) != (0, 0):
-                    arrived(daily.at[bins, chunk], day_recv.at[bins, chunk])
-                ready.append((bins, chunk))
+    for at, batch in enumerate(batches):
+        ready = [
+            (bins, NC * (((y if bins == 0 else zz) + 4 - d) % 4) + (core + dc) % NC)
+            for d, dc in batch for bins in range(SETS)
+        ]
+        coming = SETS * sum(offset != (0, 0) for offset in batch)
+        arrived(daily.at[0, pl.ds(0, coming)], day_recv.at[at])
         for bins, chunk in ready:
             stage_one(bins, chunk)
 
@@ -438,7 +440,7 @@
             DMA(()),
             DMA((SETS, 2, 4)),
             DMA(()),
-            DMA((SETS, CHUNKS)),
+            DMA((4,)),
         ],
         compiler_params=pltpu.CompilerParams(
             collective_id=0, has_side_effects=True, vmem_limit_bytes=24 << 20

time: 29.2 us -> 29.1 us (level)
  no operation moved by 1% of the time
where the time goes in v7:
time: 29.1 us; the launch traced here: 29 us
  Pallas kernels  28.2 us (97%)
  between operations  0.73 us (3%)
    pallas_call x1, Pallas kernels, body(): pl.pallas_call(kernel, out_shape=jax.ShapeDtypeStruct(middle_shape, bf16)...  26.6 us
    pallas_call x1, Pallas kernels, body(): pl.pallas_call(lags_kernel, out_shape=jax.ShapeDtypeStruct((SHARE * 3, 3,...  1.63 us

profile of v7, /device:TPU:1, one launch (start us, length us, event | category | flops | bytes accessed | tf_op | source)
XLA Modules:
  0.0 29.0 jit_solution(9868198575100198715)
XLA Ops:
  0.0 0.0 copy-start
  0.7 26.6 %correlate.1.middle = bf16[16,2,23,8,128]{4,3,2,1,0:T(8,128)(2,1)S(1)} custom-call(bf16[6,2,2048]{2,1,0:T(2,128)(2,1)} %bitcast.7, s32[2,40]{1,0:T(2,128)} %bitcast.8, bf16[128,256]{1,0:T(8,128)(2,1)} %constant.6.clone.first_hbm, f32[16,2,8,128]{3,2,1,0:T(8,128)} %constant.7.clone.twiddle_hbm), custom_call_target="tpu_custom_call" | custom-call | tf_op jit(solution)/shard_map/correlate/pallas_call | solution.py:417
  27.3 0.0 copy-done
  27.3 1.6 %lags.1 = bf16[30,3,4096]{2,1,0:T(4,128)(2,1)} custom-call(s32[1]{0:T(128)S(6)} %copy.8.count_ref, bf16[16,2,23,8,128]{4,3,2,1,0:T(8,128)(2,1)S(1)} %correlate.1.middle, bf16[2,256,512]{2,1,0:T(8,128)(2,1)S(1)} %copy-done), custom_call_target="tpu_custom_call" | custom-call | tf_op jit(solution)/shard_map/lags/pallas_call | solution.py:450
Async XLA Ops:
  0.0 27.3 %copy-start = (bf16[2,256,512]{2,1,0:T(8,128)(2,1)S(1)}, bf16[2,256,512]{2,1,0:T(8,128)(2,1)}, u32[]{:S(2)}) copy-start(bf16[2,256,512]{2,1,0:T(8,128)(2,1)} %constant.8.clone.second) | copy-start | bytes 1572868

commit v8 on v7

--- a/solution.py
+++ b/solution.py
@@ -330,7 +330,7 @@
         make(first_slot + SHARE // 4 * 4, SHARE % 4, SHARE // 4 * 9)
 
     offsets = ((2, 0), (1, 0), (3, 0), (2, 1), (1, 1), (3, 1), (0, 1))
-    batches = (((0, 0), (2, 0)), ((1, 0), (3, 0)), ((0, 1), (2, 1)), ((1, 1), (3, 1)))
+    batches = (((0, 0), (2, 0)), ((1, 0), (3, 0)), ((0, 1), (2, 1)), ((1, 1),), ((3, 1),))
     batch_of = {offset: at for at, batch in enumerate(batches) for offset in batch}
     for at, (d, dc) in enumerate(offsets):
         for bins in range(SETS):
@@ -440,7 +440,7 @@
             DMA(()),
             DMA((SETS, 2, 4)),
             DMA(()),
-            DMA((4,)),
+            DMA((5,)),
         ],
         compiler_params=pltpu.CompilerParams(
             collective_id=0, has_side_effects=True, vmem_limit_bytes=24 << 20

time: 29.1 us -> 29.3 us (level)
  no operation moved by 1% of the time
where the time goes in v8:
time: 29.3 us; the launch traced here: 29.1 us
  Pallas kernels  28.4 us (97%)
  between operations  0.73 us (2%)
    pallas_call x1, Pallas kernels, body(): pl.pallas_call(kernel, out_shape=jax.ShapeDtypeStruct(middle_shape, bf16)...  26.8 us
    pallas_call x1, Pallas kernels, body(): pl.pallas_call(lags_kernel, out_shape=jax.ShapeDtypeStruct((SHARE * 3, 3,...  1.63 us

profile of v8, /device:TPU:1, one launch (start us, length us, event | category | flops | bytes accessed | tf_op | source)
XLA Modules:
  0.0 29.1 jit_solution(6608217492962177041)
XLA Ops:
  0.0 0.0 copy-start
  0.7 26.8 %correlate.1.middle = bf16[16,2,23,8,128]{4,3,2,1,0:T(8,128)(2,1)S(1)} custom-call(bf16[6,2,2048]{2,1,0:T(2,128)(2,1)} %bitcast.7, s32[2,40]{1,0:T(2,128)} %bitcast.8, bf16[128,256]{1,0:T(8,128)(2,1)} %constant.6.clone.first_hbm, f32[16,2,8,128]{3,2,1,0:T(8,128)} %constant.7.clone.twiddle_hbm), custom_call_target="tpu_custom_call" | custom-call | tf_op jit(solution)/shard_map/correlate/pallas_call | solution.py:417
  27.5 0.0 copy-done
  27.5 1.6 %lags.1 = bf16[30,3,4096]{2,1,0:T(4,128)(2,1)} custom-call(s32[1]{0:T(128)S(6)} %copy.8.count_ref, bf16[16,2,23,8,128]{4,3,2,1,0:T(8,128)(2,1)S(1)} %correlate.1.middle, bf16[2,256,512]{2,1,0:T(8,128)(2,1)S(1)} %copy-done), custom_call_target="tpu_custom_call" | custom-call | tf_op jit(solution)/shard_map/lags/pallas_call | solution.py:450
Async XLA Ops:
  0.0 27.5 %copy-start = (bf16[2,256,512]{2,1,0:T(8,128)(2,1)S(1)}, bf16[2,256,512]{2,1,0:T(8,128)(2,1)}, u32[]{:S(2)}) copy-start(bf16[2,256,512]{2,1,0:T(8,128)(2,1)} %constant.8.clone.second) | copy-start | bytes 1572868

commit v9 on v7

--- a/solution.py
+++ b/solution.py
@@ -383,9 +383,9 @@
             for group in groups:
                 tile = 3 * group // 2
                 columns.append(jnp.concatenate(
-                    [middle[source, part, tile : tile + 2].astype(jnp.float32).reshape(16, 128)
+                    [middle[source, part, tile : tile + 2].reshape(16, 128)
                      for part in range(2) for source in range(SOURCES)], axis=0
-                ).astype(jnp.bfloat16))
+                ))
             totals = jnp.dot(
                 second[odd], jnp.concatenate(columns, axis=1), preferred_element_type=jnp.float32
             )

time: 29.1 us -> 29.1 us (level)
  no operation moved by 1% of the time
where the time goes in v9:
time: 29.1 us; the launch traced here: 29 us
  Pallas kernels  28.2 us (97%)
  between operations  0.73 us (3%)
    pallas_call x1, Pallas kernels, body(): pl.pallas_call(kernel, out_shape=jax.ShapeDtypeStruct(middle_shape, bf16)...  26.6 us
    pallas_call x1, Pallas kernels, body(): pl.pallas_call(lags_kernel, out_shape=jax.ShapeDtypeStruct((SHARE * 3, 3,...  1.63 us

profile of v9, /device:TPU:1, one launch (start us, length us, event | category | flops | bytes accessed | tf_op | source)
XLA Modules:
  0.0 29.0 jit_solution(9868198575100198715)
XLA Ops:
  0.0 0.0 copy-start
  0.7 26.6 %correlate.1.middle = bf16[16,2,23,8,128]{4,3,2,1,0:T(8,128)(2,1)S(1)} custom-call(bf16[6,2,2048]{2,1,0:T(2,128)(2,1)} %bitcast.7, s32[2,40]{1,0:T(2,128)} %bitcast.8, bf16[128,256]{1,0:T(8,128)(2,1)} %constant.6.clone.first_hbm, f32[16,2,8,128]{3,2,1,0:T(8,128)} %constant.7.clone.twiddle_hbm), custom_call_target="tpu_custom_call" | custom-call | tf_op jit(solution)/shard_map/correlate/pallas_call | solution.py:417
  27.3 0.0 copy-done
  27.3 1.6 %lags.1 = bf16[30,3,4096]{2,1,0:T(4,128)(2,1)} custom-call(s32[1]{0:T(128)S(6)} %copy.8.count_ref, bf16[16,2,23,8,128]{4,3,2,1,0:T(8,128)(2,1)S(1)} %correlate.1.middle, bf16[2,256,512]{2,1,0:T(8,128)(2,1)S(1)} %copy-done), custom_call_target="tpu_custom_call" | custom-call | tf_op jit(solution)/shard_map/lags/pallas_call | solution.py:450
Async XLA Ops:
  0.0 27.3 %copy-start = (bf16[2,256,512]{2,1,0:T(8,128)(2,1)S(1)}, bf16[2,256,512]{2,1,0:T(8,128)(2,1)}, u32[]{:S(2)}) copy-start(bf16[2,256,512]{2,1,0:T(8,128)(2,1)} %constant.8.clone.second) | copy-start | bytes 1572868
